TPU v7x, 32 devices: a whole 2x2x4 slice. The times are simulated.
32 devices in a mesh: gx: 4 (over y, x), gy: 8 (over z, core).
Axes of the slice: x: 2, y: 2, z: 4, core: 2. Of those that a mesh axis runs over, the one named last changes fastest.
Arguments:
- surface: float32 [256, 4096], P('gx', 'gy'), may hold values from -6 to 6
- east_velocity: float32 [256, 4096], P('gx', 'gy'), may hold values from -3 to 3
- north_velocity: float32 [256, 4096], P('gx', 'gy'), may hold values from -3 to 3
- east_depth: float32 [256, 4096], P('gx', 'gy'), may hold values from 0.25 to 2
- north_depth: float32 [256, 4096], P('gx', 'gy'), may hold values from 0.25 to 2
- slot_gauge: int32 [32, 128], P(('gx', 'gy')), may hold values from 0 to 2048, as said below
- slot_cell: int32 [32, 128], P(('gx', 'gy')), may hold values from 0 to 32767
Outputs:
- final_surface: float32 [256, 4096], P('gx', 'gy')
- final_east: float32 [256, 4096], P('gx', 'gy')
- final_north: float32 [256, 4096], P('gx', 'gy')
- gauge_series: float32 [2048, 48], P(('gx', 'gy'))
Inputs may be any that keep to these rules, and one draw needn't show every extreme that they name: `slot_gauge`: entries below 2048 are gauge ids: every id 0 to 2047 stands exactly once in the whole array, in the row of the device whose block holds that gauge; the ids owned by device d, d * 64 to (d + 1) * 64 - 1, all lie in blocks with d's gx index. Each row lists its ids first, then 2048 in the unused slots. Some device's row is full in every draw.
All inputs are finite; a program needn't handle non-finite values.
Results may differ from a plain program's by a relative error of at most 0.00012.
Values sent between devices are 32-bit elements; how exact they have to be, the bound alone decides.
A program may use at most 64 MiB of HBM per device.

v0:
```python
import jax
import jax.numpy as jnp
from jax import lax
from jax.sharding import PartitionSpec as P

STEPS = 16
GAUGE_DEV = 64


time_step = 0.45


def from_behind(value, axis, steps):
    count = lax.axis_size(axis)
    first, last = (max(0, -steps), min(count, count - steps))
    return lax.ppermute(value, axis, [(source, source + steps) for source in range(first, last)])


def update_velocity(eta, east, north, below, right):
    eta_down = jnp.concatenate([eta[1:], below], 0)
    eta_right = jnp.concatenate([eta[:, 1:], right], 1)
    east = east - time_step * (eta_down - eta)
    north = north - time_step * (eta_right - eta)
    return (east, north)


def update_surface(eta, flux_x, flux_y, above, left):
    flux_up = jnp.concatenate([above, flux_x[:-1]], 0)
    flux_left = jnp.concatenate([left, flux_y[:, :-1]], 1)
    return eta - time_step * (flux_x - flux_up + flux_y - flux_left)


def advance_shared(eta, east, north, east_depth, north_depth):
    below = from_behind(eta[:1], "gx", -1)
    right = from_behind(eta[:, :1], "gy", -1)
    east, north = update_velocity(eta, east, north, below, right)
    flux_x = east_depth * east
    flux_y = north_depth * north
    above = from_behind(flux_x[-1:], "gx", 1)
    left = from_behind(flux_y[:, -1:], "gy", 1)
    return (update_surface(eta, flux_x, flux_y, above, left), east, north)


def sample_cells(fields, row_pick, col_pick):
    picked = []
    for field in fields:
        rows_taken = jnp.dot(row_pick, field, precision=lax.Precision.HIGHEST)
        picked.append(jnp.sum(rows_taken * col_pick, axis=1))
    return jnp.stack(picked)


def shards(surface, east_velocity, north_velocity, east_depth, north_depth, slot_gauge, slot_cell):
    rows_dev, cols_dev = surface.shape
    slot_ids = slot_gauge.reshape(-1)
    cells = slot_cell.reshape(-1)
    count = slot_ids.shape[0]
    owner = lax.axis_index("gx") * lax.axis_size("gy") + lax.axis_index("gy")
    owned = owner * GAUGE_DEV + jnp.arange(GAUGE_DEV, dtype=jnp.int32)

    def record_step(records, step, fields, row_pick, col_pick):
        taken = sample_cells(fields, row_pick, col_pick)
        return lax.dynamic_update_slice_in_dim(records, taken[:, None, :], step, 1)

    records = jnp.zeros((3, STEPS, count), jnp.float32)
    pickers_row_pick = (
        (cells // cols_dev)[:, None] == jnp.arange(rows_dev, dtype=jnp.int32)[None, :]
    ).astype(jnp.float32)
    pickers_col_pick = (
        (cells % cols_dev)[:, None] == jnp.arange(cols_dev, dtype=jnp.int32)[None, :]
    ).astype(jnp.float32)
    row_pick = pickers_row_pick
    col_pick = pickers_col_pick

    def turn(step, carry):
        eta, east, north, kept = carry
        eta, east, north = advance_shared(eta, east, north, east_depth, north_depth)
        kept = record_step(kept, step, (eta, east, north), row_pick, col_pick)
        return (eta, east, north, kept)

    eta, east, north, records = lax.fori_loop(
        0, STEPS, turn, (surface, east_velocity, north_velocity, records)
    )
    flat_records = records.reshape(3 * STEPS, count)
    slot_rows = flat_records.T
    pooled, everyone = (
        lax.all_gather(slot_rows, "gy", axis=0, tiled=True),
        lax.all_gather(slot_ids, "gy", axis=0, tiled=True),
    )
    chooser = (owned[:, None] == everyone[None, :]).astype(jnp.float32)
    series = jnp.dot(chooser, pooled, precision=lax.Precision.HIGHEST)
    return (eta, east, north, series)


def solution(mesh):
    in_specs = (
        P("gx", "gy"),
        P("gx", "gy"),
        P("gx", "gy"),
        P("gx", "gy"),
        P("gx", "gy"),
        P(("gx", "gy"), None),
        P(("gx", "gy"), None),
    )
    out_specs = (P("gx", "gy"), P("gx", "gy"), P("gx", "gy"), P(("gx", "gy"), None))
    return jax.shard_map(shards, mesh=mesh, in_specs=in_specs, out_specs=out_specs, check_vma=False)
```

profile of v0, /device:TPU:0, one launch (start us, length us, event | category | flops | bytes accessed | tf_op | source)
XLA Modules:
  0.0 281.5 jit_solution(907743814828687567)
XLA Ops:
  1.8 254.7 %while.20 = (s32[]{:T(128)}, f32[64,512]{1,0:T(8,128)S(1)}, f32[64,512]{1,0:T(8,128)S(1)}, f32[64,512]{1,0:T(8,128)S(1)}, f32[3,16,128]{2,1,0:T(8,128)S(1)}, /*i...) while((s32[]{:T(128)}, f32[64,512]{1,0:T(8,128)S(1)}, ...), condition=%wide.region_4.5_spmd.clone, body=%wide.region_0.4_spmd.clone.sunk | while | flops 152191360 | bytes 3182873 | solution.py:80
  8.4 3.5 %collective-permute-start.3 = (f32[64,1]{1,0:T(8,128)S(1)}, f32[64,1]{1,0:T(8,128)S(1)}, u32[]{:S(2)}, u32[]{:S(2)}) collective-permute-start(f32[64,1]{1,0:T(8,128)S(1)} %slice.79), channel_id=1, source_target_pairs={{0,1},{1,2},{2,3},{3,4},{4,5},{5,6},{6,7},{8,9},{9,10},{10,11},{11... | collective-permute-start | bytes 776 | tf_op jit(solution)/shard_map/while/body/eval_jaxpr/ppermute | solution.py:16
  11.9 4.5 %collective-permute-start.2 = (f32[1,512]{1,0:T(1,128)S(1)}, f32[1,512]{1,0:T(1,128)S(1)}, u32[]{:S(2)}, u32[]{:S(2)}) collective-permute-start(f32[1,512]{1,0:T(1,128)S(1)} %slice.78), channel_id=1, source_target_pairs={{0,8},{8,16},{16,24},{1,9},{9,17},{17,25},{2,10},{10,18},{18,26},{... | collective-permute-start | bytes 6152 | tf_op jit(solution)/shard_map/while/body/eval_jaxpr/ppermute | solution.py:16
  24.7 2.7 collective-permute-start.3
  27.5 4.8 %collective-permute-start.2 = (f32[1,512]{1,0:T(1,128)S(1)}, f32[1,512]{1,0:T(1,128)S(1)}, u32[]{:S(2)}, u32[]{:S(2)}) collective-permute-start(f32[1,512]{1,0:T(1,128)S(1)} %slice.78), channel_id=1, source_target_pairs={{0,8},{8,16},{16,24},{1,9},{9,17},{17,25},{2,10},{10,18},{18,26},{... | collective-permute-start | bytes 6152 | tf_op jit(solution)/shard_map/while/body/eval_jaxpr/ppermute | solution.py:16
  41.2 2.7 collective-permute-start.3
  44.0 4.8 %collective-permute-start.2 = (f32[1,512]{1,0:T(1,128)S(1)}, f32[1,512]{1,0:T(1,128)S(1)}, u32[]{:S(2)}, u32[]{:S(2)}) collective-permute-start(f32[1,512]{1,0:T(1,128)S(1)} %slice.78), channel_id=1, source_target_pairs={{0,8},{8,16},{16,24},{1,9},{9,17},{17,25},{2,10},{10,18},{18,26},{... | collective-permute-start | bytes 6152 | tf_op jit(solution)/shard_map/while/body/eval_jaxpr/ppermute | solution.py:16
  57.8 2.7 collective-permute-start.3
  60.5 4.6 %collective-permute-start.2 = (f32[1,512]{1,0:T(1,128)S(1)}, f32[1,512]{1,0:T(1,128)S(1)}, u32[]{:S(2)}, u32[]{:S(2)}) collective-permute-start(f32[1,512]{1,0:T(1,128)S(1)} %slice.78), channel_id=1, source_target_pairs={{0,8},{8,16},{16,24},{1,9},{9,17},{17,25},{2,10},{10,18},{18,26},{... | collective-permute-start | bytes 6152 | tf_op jit(solution)/shard_map/while/body/eval_jaxpr/ppermute | solution.py:16
  73.5 2.7 collective-permute-start.3
  76.3 4.6 %collective-permute-start.2 = (f32[1,512]{1,0:T(1,128)S(1)}, f32[1,512]{1,0:T(1,128)S(1)}, u32[]{:S(2)}, u32[]{:S(2)}) collective-permute-start(f32[1,512]{1,0:T(1,128)S(1)} %slice.78), channel_id=1, source_target_pairs={{0,8},{8,16},{16,24},{1,9},{9,17},{17,25},{2,10},{10,18},{18,26},{... | collective-permute-start | bytes 6152 | tf_op jit(solution)/shard_map/while/body/eval_jaxpr/ppermute | solution.py:16
  92.1 4.6 %collective-permute-start.2 = (f32[1,512]{1,0:T(1,128)S(1)}, f32[1,512]{1,0:T(1,128)S(1)}, u32[]{:S(2)}, u32[]{:S(2)}) collective-permute-start(f32[1,512]{1,0:T(1,128)S(1)} %slice.78), channel_id=1, source_target_pairs={{0,8},{8,16},{16,24},{1,9},{9,17},{17,25},{2,10},{10,18},{18,26},{... | collective-permute-start | bytes 6152 | tf_op jit(solution)/shard_map/while/body/eval_jaxpr/ppermute | solution.py:16
  107.8 4.6 %collective-permute-start.2 = (f32[1,512]{1,0:T(1,128)S(1)}, f32[1,512]{1,0:T(1,128)S(1)}, u32[]{:S(2)}, u32[]{:S(2)}) collective-permute-start(f32[1,512]{1,0:T(1,128)S(1)} %slice.78), channel_id=1, source_target_pairs={{0,8},{8,16},{16,24},{1,9},{9,17},{17,25},{2,10},{10,18},{18,26},{... | collective-permute-start | bytes 6152 | tf_op jit(solution)/shard_map/while/body/eval_jaxpr/ppermute | solution.py:16
  123.6 4.6 %collective-permute-start.2 = (f32[1,512]{1,0:T(1,128)S(1)}, f32[1,512]{1,0:T(1,128)S(1)}, u32[]{:S(2)}, u32[]{:S(2)}) collective-permute-start(f32[1,512]{1,0:T(1,128)S(1)} %slice.78), channel_id=1, source_target_pairs={{0,8},{8,16},{16,24},{1,9},{9,17},{17,25},{2,10},{10,18},{18,26},{... | collective-permute-start | bytes 6152 | tf_op jit(solution)/shard_map/while/body/eval_jaxpr/ppermute | solution.py:16
  139.4 4.6 %collective-permute-start.2 = (f32[1,512]{1,0:T(1,128)S(1)}, f32[1,512]{1,0:T(1,128)S(1)}, u32[]{:S(2)}, u32[]{:S(2)}) collective-permute-start(f32[1,512]{1,0:T(1,128)S(1)} %slice.78), channel_id=1, source_target_pairs={{0,8},{8,16},{16,24},{1,9},{9,17},{17,25},{2,10},{10,18},{18,26},{... | collective-permute-start | bytes 6152 | tf_op jit(solution)/shard_map/while/body/eval_jaxpr/ppermute | solution.py:16
  155.2 4.6 %collective-permute-start.2 = (f32[1,512]{1,0:T(1,128)S(1)}, f32[1,512]{1,0:T(1,128)S(1)}, u32[]{:S(2)}, u32[]{:S(2)}) collective-permute-start(f32[1,512]{1,0:T(1,128)S(1)} %slice.78), channel_id=1, source_target_pairs={{0,8},{8,16},{16,24},{1,9},{9,17},{17,25},{2,10},{10,18},{18,26},{... | collective-permute-start | bytes 6152 | tf_op jit(solution)/shard_map/while/body/eval_jaxpr/ppermute | solution.py:16
  170.9 4.6 %collective-permute-start.2 = (f32[1,512]{1,0:T(1,128)S(1)}, f32[1,512]{1,0:T(1,128)S(1)}, u32[]{:S(2)}, u32[]{:S(2)}) collective-permute-start(f32[1,512]{1,0:T(1,128)S(1)} %slice.78), channel_id=1, source_target_pairs={{0,8},{8,16},{16,24},{1,9},{9,17},{17,25},{2,10},{10,18},{18,26},{... | collective-permute-start | bytes 6152 | tf_op jit(solution)/shard_map/while/body/eval_jaxpr/ppermute | solution.py:16
  186.7 4.6 %collective-permute-start.2 = (f32[1,512]{1,0:T(1,128)S(1)}, f32[1,512]{1,0:T(1,128)S(1)}, u32[]{:S(2)}, u32[]{:S(2)}) collective-permute-start(f32[1,512]{1,0:T(1,128)S(1)} %slice.78), channel_id=1, source_target_pairs={{0,8},{8,16},{16,24},{1,9},{9,17},{17,25},{2,10},{10,18},{18,26},{... | collective-permute-start | bytes 6152 | tf_op jit(solution)/shard_map/while/body/eval_jaxpr/ppermute | solution.py:16
  202.5 4.6 %collective-permute-start.2 = (f32[1,512]{1,0:T(1,128)S(1)}, f32[1,512]{1,0:T(1,128)S(1)}, u32[]{:S(2)}, u32[]{:S(2)}) collective-permute-start(f32[1,512]{1,0:T(1,128)S(1)} %slice.78), channel_id=1, source_target_pairs={{0,8},{8,16},{16,24},{1,9},{9,17},{17,25},{2,10},{10,18},{18,26},{... | collective-permute-start | bytes 6152 | tf_op jit(solution)/shard_map/while/body/eval_jaxpr/ppermute | solution.py:16
  218.3 4.6 %collective-permute-start.2 = (f32[1,512]{1,0:T(1,128)S(1)}, f32[1,512]{1,0:T(1,128)S(1)}, u32[]{:S(2)}, u32[]{:S(2)}) collective-permute-start(f32[1,512]{1,0:T(1,128)S(1)} %slice.78), channel_id=1, source_target_pairs={{0,8},{8,16},{16,24},{1,9},{9,17},{17,25},{2,10},{10,18},{18,26},{... | collective-permute-start | bytes 6152 | tf_op jit(solution)/shard_map/while/body/eval_jaxpr/ppermute | solution.py:16
  234.0 4.6 %collective-permute-start.2 = (f32[1,512]{1,0:T(1,128)S(1)}, f32[1,512]{1,0:T(1,128)S(1)}, u32[]{:S(2)}, u32[]{:S(2)}) collective-permute-start(f32[1,512]{1,0:T(1,128)S(1)} %slice.78), channel_id=1, source_target_pairs={{0,8},{8,16},{16,24},{1,9},{9,17},{17,25},{2,10},{10,18},{18,26},{... | collective-permute-start | bytes 6152 | tf_op jit(solution)/shard_map/while/body/eval_jaxpr/ppermute | solution.py:16
  249.8 4.6 %collective-permute-start.2 = (f32[1,512]{1,0:T(1,128)S(1)}, f32[1,512]{1,0:T(1,128)S(1)}, u32[]{:S(2)}, u32[]{:S(2)}) collective-permute-start(f32[1,512]{1,0:T(1,128)S(1)} %slice.78), channel_id=1, source_target_pairs={{0,8},{8,16},{16,24},{1,9},{9,17},{17,25},{2,10},{10,18},{18,26},{... | collective-permute-start | bytes 6152 | tf_op jit(solution)/shard_map/while/body/eval_jaxpr/ppermute | solution.py:16
  256.6 14.1 %all_gather.7 = f32[1024,48]{0,1:T(8,128)S(1)} all-gather(f32[128,48]{0,1:T(8,128)S(1)} %bitcast.74), channel_id=1, replica_groups=mesh['gx'=4,'gy'=8] {'gy'}, dimensions={0}, use_global_device_ids=true | all-gather | bytes 221184 | tf_op jit(solution)/shard_map/all_gather | solution.py:86
  271.3 9.2 %all-gather = s32[1,1024]{1,0:T(1,128)S(1)} all-gather(s32[1,128]{1,0:T(1,128)S(1)} %copy-done.8), channel_id=2, replica_groups=mesh['gx'=4,'gy'=8] {'gy'}, dimensions={1}, use_global_device_ids=true | all-gather | bytes 4608 | tf_op jit(solution)/shard_map/all_gather | solution.py:87
  (355 shorter events, 167.8 us)
Async XLA Ops:
  1.8 6.4 %collective-permute-start = (f32[1,512]{1,0:T(1,128)S(1)}, f32[1,512]{1,0:T(1,128)S(1)}, u32[]{:S(2)}, u32[]{:S(2)}) collective-permute-start(f32[1,512]{1,0:T(1,128)S(1)} %slice.74), channel_id=1, source_target_pairs={{8,0},{16,8},{24,16},{9,1},{17,9},{25,17},{10,2},{18,10},{26,18},{... | collective-permute-start | bytes 6152 | tf_op jit(solution)/shard_map/while/body/eval_jaxpr/ppermute | solution.py:16
  8.4 9.3 %collective-permute-start.3 = (f32[64,1]{1,0:T(8,128)S(1)}, f32[64,1]{1,0:T(8,128)S(1)}, u32[]{:S(2)}, u32[]{:S(2)}) collective-permute-start(f32[64,1]{1,0:T(8,128)S(1)} %slice.79), channel_id=1, source_target_pairs={{0,1},{1,2},{2,3},{3,4},{4,5},{5,6},{6,7},{8,9},{9,10},{10,11},{11... | collective-permute-start | bytes 776 | tf_op jit(solution)/shard_map/while/body/eval_jaxpr/ppermute | solution.py:16
  24.7 8.8 %collective-permute-start.3 = (f32[64,1]{1,0:T(8,128)S(1)}, f32[64,1]{1,0:T(8,128)S(1)}, u32[]{:S(2)}, u32[]{:S(2)}) collective-permute-start(f32[64,1]{1,0:T(8,128)S(1)} %slice.79), channel_id=1, source_target_pairs={{0,1},{1,2},{2,3},{3,4},{4,5},{5,6},{6,7},{8,9},{9,10},{10,11},{11... | collective-permute-start | bytes 776 | tf_op jit(solution)/shard_map/while/body/eval_jaxpr/ppermute | solution.py:16
  34.4 6.6 %collective-permute-start = (f32[1,512]{1,0:T(1,128)S(1)}, f32[1,512]{1,0:T(1,128)S(1)}, u32[]{:S(2)}, u32[]{:S(2)}) collective-permute-start(f32[1,512]{1,0:T(1,128)S(1)} %slice.74), channel_id=1, source_target_pairs={{8,0},{16,8},{24,16},{9,1},{17,9},{25,17},{10,2},{18,10},{26,18},{... | collective-permute-start | bytes 6152 | tf_op jit(solution)/shard_map/while/body/eval_jaxpr/ppermute | solution.py:16
  41.2 8.8 %collective-permute-start.3 = (f32[64,1]{1,0:T(8,128)S(1)}, f32[64,1]{1,0:T(8,128)S(1)}, u32[]{:S(2)}, u32[]{:S(2)}) collective-permute-start(f32[64,1]{1,0:T(8,128)S(1)} %slice.79), channel_id=1, source_target_pairs={{0,1},{1,2},{2,3},{3,4},{4,5},{5,6},{6,7},{8,9},{9,10},{10,11},{11... | collective-permute-start | bytes 776 | tf_op jit(solution)/shard_map/while/body/eval_jaxpr/ppermute | solution.py:16
  50.9 6.6 %collective-permute-start = (f32[1,512]{1,0:T(1,128)S(1)}, f32[1,512]{1,0:T(1,128)S(1)}, u32[]{:S(2)}, u32[]{:S(2)}) collective-permute-start(f32[1,512]{1,0:T(1,128)S(1)} %slice.74), channel_id=1, source_target_pairs={{8,0},{16,8},{24,16},{9,1},{17,9},{25,17},{10,2},{18,10},{26,18},{... | collective-permute-start | bytes 6152 | tf_op jit(solution)/shard_map/while/body/eval_jaxpr/ppermute | solution.py:16
  57.8 8.6 %collective-permute-start.3 = (f32[64,1]{1,0:T(8,128)S(1)}, f32[64,1]{1,0:T(8,128)S(1)}, u32[]{:S(2)}, u32[]{:S(2)}) collective-permute-start(f32[64,1]{1,0:T(8,128)S(1)} %slice.79), channel_id=1, source_target_pairs={{0,1},{1,2},{2,3},{3,4},{4,5},{5,6},{6,7},{8,9},{9,10},{10,11},{11... | collective-permute-start | bytes 776 | tf_op jit(solution)/shard_map/while/body/eval_jaxpr/ppermute | solution.py:16
  73.5 8.6 %collective-permute-start.3 = (f32[64,1]{1,0:T(8,128)S(1)}, f32[64,1]{1,0:T(8,128)S(1)}, u32[]{:S(2)}, u32[]{:S(2)}) collective-permute-start(f32[64,1]{1,0:T(8,128)S(1)} %slice.79), channel_id=1, source_target_pairs={{0,1},{1,2},{2,3},{3,4},{4,5},{5,6},{6,7},{8,9},{9,10},{10,11},{11... | collective-permute-start | bytes 776 | tf_op jit(solution)/shard_map/while/body/eval_jaxpr/ppermute | solution.py:16
  83.0 6.1 %collective-permute-start = (f32[1,512]{1,0:T(1,128)S(1)}, f32[1,512]{1,0:T(1,128)S(1)}, u32[]{:S(2)}, u32[]{:S(2)}) collective-permute-start(f32[1,512]{1,0:T(1,128)S(1)} %slice.74), channel_id=1, source_target_pairs={{8,0},{16,8},{24,16},{9,1},{17,9},{25,17},{10,2},{18,10},{26,18},{... | collective-permute-start | bytes 6152 | tf_op jit(solution)/shard_map/while/body/eval_jaxpr/ppermute | solution.py:16
  89.3 8.6 %collective-permute-start.3 = (f32[64,1]{1,0:T(8,128)S(1)}, f32[64,1]{1,0:T(8,128)S(1)}, u32[]{:S(2)}, u32[]{:S(2)}) collective-permute-start(f32[64,1]{1,0:T(8,128)S(1)} %slice.79), channel_id=1, source_target_pairs={{0,1},{1,2},{2,3},{3,4},{4,5},{5,6},{6,7},{8,9},{9,10},{10,11},{11... | collective-permute-start | bytes 776 | tf_op jit(solution)/shard_map/while/body/eval_jaxpr/ppermute | solution.py:16
  105.1 8.6 %collective-permute-start.3 = (f32[64,1]{1,0:T(8,128)S(1)}, f32[64,1]{1,0:T(8,128)S(1)}, u32[]{:S(2)}, u32[]{:S(2)}) collective-permute-start(f32[64,1]{1,0:T(8,128)S(1)} %slice.79), channel_id=1, source_target_pairs={{0,1},{1,2},{2,3},{3,4},{4,5},{5,6},{6,7},{8,9},{9,10},{10,11},{11... | collective-permute-start | bytes 776 | tf_op jit(solution)/shard_map/while/body/eval_jaxpr/ppermute | solution.py:16
  120.9 8.6 %collective-permute-start.3 = (f32[64,1]{1,0:T(8,128)S(1)}, f32[64,1]{1,0:T(8,128)S(1)}, u32[]{:S(2)}, u32[]{:S(2)}) collective-permute-start(f32[64,1]{1,0:T(8,128)S(1)} %slice.79), channel_id=1, source_target_pairs={{0,1},{1,2},{2,3},{3,4},{4,5},{5,6},{6,7},{8,9},{9,10},{10,11},{11... | collective-permute-start | bytes 776 | tf_op jit(solution)/shard_map/while/body/eval_jaxpr/ppermute | solution.py:16
  130.4 6.1 %collective-permute-start = (f32[1,512]{1,0:T(1,128)S(1)}, f32[1,512]{1,0:T(1,128)S(1)}, u32[]{:S(2)}, u32[]{:S(2)}) collective-permute-start(f32[1,512]{1,0:T(1,128)S(1)} %slice.74), channel_id=1, source_target_pairs={{8,0},{16,8},{24,16},{9,1},{17,9},{25,17},{10,2},{18,10},{26,18},{... | collective-permute-start | bytes 6152 | tf_op jit(solution)/shard_map/while/body/eval_jaxpr/ppermute | solution.py:16
  136.7 8.6 %collective-permute-start.3 = (f32[64,1]{1,0:T(8,128)S(1)}, f32[64,1]{1,0:T(8,128)S(1)}, u32[]{:S(2)}, u32[]{:S(2)}) collective-permute-start(f32[64,1]{1,0:T(8,128)S(1)} %slice.79), channel_id=1, source_target_pairs={{0,1},{1,2},{2,3},{3,4},{4,5},{5,6},{6,7},{8,9},{9,10},{10,11},{11... | collective-permute-start | bytes 776 | tf_op jit(solution)/shard_map/while/body/eval_jaxpr/ppermute | solution.py:16
  152.4 8.6 %collective-permute-start.3 = (f32[64,1]{1,0:T(8,128)S(1)}, f32[64,1]{1,0:T(8,128)S(1)}, u32[]{:S(2)}, u32[]{:S(2)}) collective-permute-start(f32[64,1]{1,0:T(8,128)S(1)} %slice.79), channel_id=1, source_target_pairs={{0,1},{1,2},{2,3},{3,4},{4,5},{5,6},{6,7},{8,9},{9,10},{10,11},{11... | collective-permute-start | bytes 776 | tf_op jit(solution)/shard_map/while/body/eval_jaxpr/ppermute | solution.py:16
  168.2 8.6 %collective-permute-start.3 = (f32[64,1]{1,0:T(8,128)S(1)}, f32[64,1]{1,0:T(8,128)S(1)}, u32[]{:S(2)}, u32[]{:S(2)}) collective-permute-start(f32[64,1]{1,0:T(8,128)S(1)} %slice.79), channel_id=1, source_target_pairs={{0,1},{1,2},{2,3},{3,4},{4,5},{5,6},{6,7},{8,9},{9,10},{10,11},{11... | collective-permute-start | bytes 776 | tf_op jit(solution)/shard_map/while/body/eval_jaxpr/ppermute | solution.py:16
  177.7 6.1 %collective-permute-start = (f32[1,512]{1,0:T(1,128)S(1)}, f32[1,512]{1,0:T(1,128)S(1)}, u32[]{:S(2)}, u32[]{:S(2)}) collective-permute-start(f32[1,512]{1,0:T(1,128)S(1)} %slice.74), channel_id=1, source_target_pairs={{8,0},{16,8},{24,16},{9,1},{17,9},{25,17},{10,2},{18,10},{26,18},{... | collective-permute-start | bytes 6152 | tf_op jit(solution)/shard_map/while/body/eval_jaxpr/ppermute | solution.py:16
  184.0 8.6 %collective-permute-start.3 = (f32[64,1]{1,0:T(8,128)S(1)}, f32[64,1]{1,0:T(8,128)S(1)}, u32[]{:S(2)}, u32[]{:S(2)}) collective-permute-start(f32[64,1]{1,0:T(8,128)S(1)} %slice.79), channel_id=1, source_target_pairs={{0,1},{1,2},{2,3},{3,4},{4,5},{5,6},{6,7},{8,9},{9,10},{10,11},{11... | collective-permute-start | bytes 776 | tf_op jit(solution)/shard_map/while/body/eval_jaxpr/ppermute | solution.py:16
  193.5 6.1 %collective-permute-start = (f32[1,512]{1,0:T(1,128)S(1)}, f32[1,512]{1,0:T(1,128)S(1)}, u32[]{:S(2)}, u32[]{:S(2)}) collective-permute-start(f32[1,512]{1,0:T(1,128)S(1)} %slice.74), channel_id=1, source_target_pairs={{8,0},{16,8},{24,16},{9,1},{17,9},{25,17},{10,2},{18,10},{26,18},{... | collective-permute-start | bytes 6152 | tf_op jit(solution)/shard_map/while/body/eval_jaxpr/ppermute | solution.py:16
  199.8 8.6 %collective-permute-start.3 = (f32[64,1]{1,0:T(8,128)S(1)}, f32[64,1]{1,0:T(8,128)S(1)}, u32[]{:S(2)}, u32[]{:S(2)}) collective-permute-start(f32[64,1]{1,0:T(8,128)S(1)} %slice.79), channel_id=1, source_target_pairs={{0,1},{1,2},{2,3},{3,4},{4,5},{5,6},{6,7},{8,9},{9,10},{10,11},{11... | collective-permute-start | bytes 776 | tf_op jit(solution)/shard_map/while/body/eval_jaxpr/ppermute | solution.py:16
  215.5 8.6 %collective-permute-start.3 = (f32[64,1]{1,0:T(8,128)S(1)}, f32[64,1]{1,0:T(8,128)S(1)}, u32[]{:S(2)}, u32[]{:S(2)}) collective-permute-start(f32[64,1]{1,0:T(8,128)S(1)} %slice.79), channel_id=1, source_target_pairs={{0,1},{1,2},{2,3},{3,4},{4,5},{5,6},{6,7},{8,9},{9,10},{10,11},{11... | collective-permute-start | bytes 776 | tf_op jit(solution)/shard_map/while/body/eval_jaxpr/ppermute | solution.py:16
  225.0 6.1 %collective-permute-start = (f32[1,512]{1,0:T(1,128)S(1)}, f32[1,512]{1,0:T(1,128)S(1)}, u32[]{:S(2)}, u32[]{:S(2)}) collective-permute-start(f32[1,512]{1,0:T(1,128)S(1)} %slice.74), channel_id=1, source_target_pairs={{8,0},{16,8},{24,16},{9,1},{17,9},{25,17},{10,2},{18,10},{26,18},{... | collective-permute-start | bytes 6152 | tf_op jit(solution)/shard_map/while/body/eval_jaxpr/ppermute | solution.py:16
  231.3 8.6 %collective-permute-start.3 = (f32[64,1]{1,0:T(8,128)S(1)}, f32[64,1]{1,0:T(8,128)S(1)}, u32[]{:S(2)}, u32[]{:S(2)}) collective-permute-start(f32[64,1]{1,0:T(8,128)S(1)} %slice.79), channel_id=1, source_target_pairs={{0,1},{1,2},{2,3},{3,4},{4,5},{5,6},{6,7},{8,9},{9,10},{10,11},{11... | collective-permute-start | bytes 776 | tf_op jit(solution)/shard_map/while/body/eval_jaxpr/ppermute | solution.py:16
  247.1 8.6 %collective-permute-start.3 = (f32[64,1]{1,0:T(8,128)S(1)}, f32[64,1]{1,0:T(8,128)S(1)}, u32[]{:S(2)}, u32[]{:S(2)}) collective-permute-start(f32[64,1]{1,0:T(8,128)S(1)} %slice.79), channel_id=1, source_target_pairs={{0,1},{1,2},{2,3},{3,4},{4,5},{5,6},{6,7},{8,9},{9,10},{10,11},{11... | collective-permute-start | bytes 776 | tf_op jit(solution)/shard_map/while/body/eval_jaxpr/ppermute | solution.py:16
  (50 other events, 274.4 us)
where the time goes:
time: 285 us; the launch traced here: 281 us
  starting transfers between devices  159 us (56%)
  waiting for transfers between devices  55.1 us (19%)
  matrix products  32 us (11%)
  blocking collectives  23.3 us (8%)
  local copies, waits for them, and re-layouts  5.67 us (2%)
  other arithmetic  4.07 us (1%)
    ppermute x64, starting transfers between devices, from_behind(): lax.ppermute(value, axis, [(source, source + steps) for source in range(f...  159 us
    ppermute x64, waiting for transfers between devices, from_behind(): lax.ppermute(value, axis, [(source, source + steps) for source in range(f...  55.1 us
    dot_general x48, matrix products, sample_cells(): rows_taken = jnp.dot(row_pick, field, precision=lax.Precision.HIGHEST)  31 us
    all_gather x1, blocking collectives, shards(): lax.all_gather(slot_rows, 'gy', axis=0, tiled=True)  14.1 us
    all_gather x1, blocking collectives, shards(): lax.all_gather(slot_ids, 'gy', axis=0, tiled=True)  9.22 us
  transfers between devices with their start and end apart: 64, of which 32 were waited for; matrix products, arithmetic and copies ran while one was open for 8% of the time, Pallas kernels for 0%

commit v1 on v0

v1 whole, which is shorter than its diff:
```python
import jax
import jax.numpy as jnp
from jax import lax
from jax.experimental import pallas as pl
from jax.experimental.pallas import tpu as pltpu
from jax.sharding import PartitionSpec as P

STEPS = 16
GAUGE_DEV = 64
LANES = 128
HALO = STEPS
time_step = 0.45
MESH = pl.DeviceIdType.MESH


def kernel(
    n_gx, n_gy, eta_hbm, east_hbm, north_hbm, hx_hbm, hy_hbm, ids_ref, cell_ref,
    eta_out, east_out, north_out, series_out,
    wide, hist, packed, sides, final_eta, outbox, inbox, series_buf,
    load_sem, row_send, row_recv, col_send, col_recv, corner_send, corner_recv,
    mail_send, mail_recv, out_sem,
):
    rows, cols = eta_hbm.shape
    chunks = cols // LANES
    tall = rows + 2 * HALO
    plane = (chunks + 1) * tall
    a, b = lax.axis_index("gx"), lax.axis_index("gy")
    has_up, has_down = a > 0, a < n_gx - 1
    has_left, has_right = b > 0, b < n_gy - 1

    loads = []
    for f, src in enumerate((eta_hbm, east_hbm, north_hbm, hx_hbm, hy_hbm)):
        for c in range(chunks):
            copy = pltpu.make_async_copy(
                src.at[:, c * LANES:(c + 1) * LANES],
                wide.at[f, c, HALO:HALO + rows, :], load_sem.at[f, c])
            copy.start()
            loads.append(copy)

    zero_rows = jnp.zeros((5, chunks, HALO, LANES), jnp.float32)
    zero_side = jnp.zeros((tall, LANES), jnp.float32)
    zero_cap = jnp.zeros((2, HALO, LANES), jnp.float32)

    @pl.when(jnp.logical_not(has_up))
    def _():
        wide[:, 0:chunks, 0:HALO, :] = zero_rows
        sides[:, 0:HALO, :] = zero_cap

    @pl.when(jnp.logical_not(has_down))
    def _():
        wide[:, 0:chunks, HALO + rows:tall, :] = zero_rows
        sides[:, HALO + rows:tall, :] = zero_cap

    @pl.when(jnp.logical_not(has_left))
    def _():
        sides[0, HALO:HALO + rows, :] = zero_side[:rows]

    @pl.when(jnp.logical_not(has_right))
    def _():
        sides[1, HALO:HALO + rows, :] = zero_side[:rows]

    barrier = pltpu.get_barrier_semaphore()

    @pl.when(has_up)
    def _():
        pl.semaphore_signal(barrier, inc=1, device_id=(a - 1, b), device_id_type=MESH)

    @pl.when(has_down)
    def _():
        pl.semaphore_signal(barrier, inc=1, device_id=(a + 1, b), device_id_type=MESH)

    for d in range(1, n_gy):
        pl.semaphore_signal(barrier, inc=1, device_id=(a, lax.rem(b + d, n_gy)), device_id_type=MESH)
    pl.semaphore_wait(
        barrier, n_gy - 1 + has_up.astype(jnp.int32) + has_down.astype(jnp.int32))

    for copy in loads:
        copy.wait()

    def row_copy(k):
        source = (HALO, rows)[k]
        target = (HALO + rows, 0)[k]
        return pltpu.make_async_remote_copy(
            wide.at[:, 0:chunks, source:source + HALO, :],
            wide.at[:, 0:chunks, target:target + HALO, :],
            row_send.at[k], row_recv.at[k],
            device_id=(a + (-1, 1)[k], b), device_id_type=MESH)

    def corner_copy(k):
        source = (HALO, rows)[k]
        target = (HALO + rows, 0)[k]
        return pltpu.make_async_remote_copy(
            sides.at[:, source:source + HALO, :], sides.at[:, target:target + HALO, :],
            corner_send.at[k], corner_recv.at[k],
            device_id=(a + (-1, 1)[k], b), device_id_type=MESH)

    def col_copy(k):
        return pltpu.make_async_remote_copy(
            packed.at[k], sides.at[k, HALO:HALO + rows, :],
            col_send.at[k], col_recv.at[k],
            device_id=(a, b + (1, -1)[k]), device_id_type=MESH)

    lane = lax.broadcasted_iota(jnp.int32, (rows, LANES), 1)
    for k in range(2):
        total = jnp.zeros((rows, LANES), jnp.float32)
        for f in range(5):
            tile = wide[f, (chunks - 1, 0)[k], HALO:HALO + rows, :]
            shift = (f * HALO + (HALO, 0)[k]) % LANES
            moved = pltpu.roll(tile, shift, axis=1) if shift else tile
            total = jnp.where((lane >= f * HALO) & (lane < (f + 1) * HALO), moved, total)
        packed[k] = total

    @pl.when(has_right)
    def _():
        col_copy(0).start()

    @pl.when(has_left)
    def _():
        col_copy(1).start()

    @pl.when(has_up)
    def _():
        row_copy(0).start()

    @pl.when(has_down)
    def _():
        row_copy(1).start()

    @pl.when(has_right)
    def _():
        col_copy(0).wait_send()
        col_copy(1).wait_recv()

    @pl.when(has_left)
    def _():
        col_copy(1).wait_send()
        col_copy(0).wait_recv()

    @pl.when(has_up)
    def _():
        corner_copy(0).start()

    @pl.when(has_down)
    def _():
        corner_copy(1).start()

    @pl.when(has_up)
    def _():
        row_copy(0).wait_send()
        row_copy(1).wait_recv()
        corner_copy(0).wait_send()
        corner_copy(1).wait_recv()

    @pl.when(has_down)
    def _():
        row_copy(1).wait_send()
        row_copy(0).wait_recv()
        corner_copy(1).wait_send()
        corner_copy(0).wait_recv()

    lane = lax.broadcasted_iota(jnp.int32, (tall, LANES), 1)
    scales = (time_step, 1.0, 1.0, time_step * time_step, time_step * time_step)
    for f in range(5):
        for c in range(chunks + 1):
            if c < chunks:
                tile = wide[f, c]
            else:
                left, right = sides[0], sides[1]
                left = pltpu.roll(left, (LANES - HALO - f * HALO) % LANES, axis=1)
                if f:
                    right = pltpu.roll(right, (LANES - f * HALO) % LANES, axis=1)
                tile = jnp.where(lane < HALO, right, jnp.where(lane >= LANES - HALO, left, 0.0))
            if f in (0, 3, 4):
                tile = tile * scales[f]
            if f < 3:
                start = f * (STEPS + 1) * plane + c * tall
                hist[start:start + tall, :] = tile
            else:
                wide[f, c] = tile

    keep_row = has_down.astype(jnp.float32)
    keep_col = has_right.astype(jnp.float32)
    first_lane, last_lane = lane == 0, lane == LANES - 1
    side_mask = jnp.where(lane < LANES // 2, keep_col, 1.0)

    def step(s, carry):
        def at(f, c, t):
            return pl.ds(pl.multiple_of((f * (STEPS + 1) + t) * plane + c * tall, 8), tall)

        def put_eta(c, new):
            base = pl.multiple_of((s + 1) * plane + c * tall, 8)
            if c == chunks:
                new = new * side_mask
            hist[pl.ds(base, HALO + rows), :] = new[:HALO + rows]
            hist[pl.ds(base + HALO + rows, HALO), :] = new[HALO + rows:] * keep_row

        def rolled_eta(c):
            return pltpu.roll(hist[at(0, c, s), :], LANES - 1, axis=1)

        order = [chunks] + list(range(chunks))
        rolled = rolled_eta(chunks)
        held = None
        behind = None
        for c in order:
            after = rolled_eta((c + 1) % (chunks + 1))
            eta = hist[at(0, c, s), :]
            east = hist[at(1, c, s), :] - (pltpu.roll(eta, tall - 1, axis=0) - eta)
            north = hist[at(2, c, s), :] - (jnp.where(last_lane, after, rolled) - eta)
            hist[at(1, c, s + 1), :] = east
            hist[at(2, c, s + 1), :] = north
            fx = wide[3, c] * east
            fy = wide[4, c] * north
            part = eta - (fx - pltpu.roll(fx, 1, axis=0)) - fy
            moved = pltpu.roll(fy, 1, axis=1)
            if c == chunks:
                held = (part, moved)
            else:
                put_eta(c, part + jnp.where(first_lane, behind, moved))
            behind = moved
            rolled = after
        part, moved = held
        put_eta(chunks, part + jnp.where(first_lane, behind, moved))
        return carry

    lax.fori_loop(0, STEPS, step, 0)

    outs = []
    for c in range(chunks):
        start = STEPS * plane + c * tall + HALO
        final_eta[c] = hist[start:start + rows, :] * (1.0 / time_step)
        where_out = pl.ds(c * LANES, LANES)
        outs.append(pltpu.make_async_copy(final_eta.at[c], eta_out.at[:, where_out], out_sem.at[0, c]))
        for f, dst in ((1, east_out), (2, north_out)):
            start = (f * (STEPS + 1) + STEPS) * plane + c * tall + HALO
            outs.append(pltpu.make_async_copy(
                hist.at[start:start + rows, :], dst.at[:, where_out], out_sem.at[f, c]))
    for copy in outs:
        copy.start()

    slots = ids_ref.shape[1]
    slot_lane = lax.broadcasted_iota(jnp.int32, (STEPS, slots), 1)

    def pick(k, kept):
        cell = cell_ref[0, k]
        row = cell // cols
        col = cell - row * cols
        chunk = col // LANES
        here = col - chunk * LANES
        start = plane + chunk * tall + HALO + row
        shift = lax.rem(k - here + LANES, LANES)
        new = []
        for f in range(3):
            slab = hist[pl.ds(f * (STEPS + 1) * plane + start, STEPS, stride=plane), :]
            slab = pltpu.roll(slab, shift, axis=1)
            new.append(jnp.where(slot_lane == k, slab, kept[f]))
        return tuple(new)

    blank = jnp.zeros((STEPS, slots), jnp.float32)
    kept = lax.fori_loop(0, slots, pick, (blank, blank, blank), unroll=8)
    records = jnp.concatenate([kept[0] * (1.0 / time_step), kept[1], kept[2]], 0)
    half = 3 * STEPS // 2
    pair = jnp.concatenate([records[:half], records[half:]], 1)
    high = pair.astype(jnp.bfloat16)
    rest = pair - high.astype(jnp.float32)
    middle = rest.astype(jnp.bfloat16)
    low = (rest - middle.astype(jnp.float32)).astype(jnp.bfloat16)
    local_ids = ids_ref[...] - a * (n_gy * GAUGE_DEV)
    entry = lax.broadcasted_iota(jnp.int32, (2 * GAUGE_DEV, slots), 0)
    for o in range(n_gy):
        lower = (entry < GAUGE_DEV) & (local_ids == entry + o * GAUGE_DEV)
        upper = (entry >= GAUGE_DEV) & (local_ids == entry + (o - 1) * GAUGE_DEV)
        chooser = jnp.concatenate(
            [jnp.where(lower, 1.0, 0.0), jnp.where(upper, 1.0, 0.0)], 1).astype(jnp.bfloat16)
        total = None
        for piece in (low, middle, high):
            got = lax.dot_general(piece, chooser, (((1,), (1,)), ((), ())),
                                  preferred_element_type=jnp.float32)
            total = got if total is None else total + got
        outbox[o] = total

    def mail(d):
        peer = lax.rem(b + d, n_gy)
        return pltpu.make_async_remote_copy(
            outbox.at[peer], inbox.at[d], mail_send.at[d], mail_recv.at[d],
            device_id=(a, peer), device_id_type=MESH)

    for d in range(1, n_gy):
        mail(d).start()
    total = outbox[b]
    for d in range(1, n_gy):
        mail(d).wait_recv()
        total = total + inbox[d]
    flipped = total.T
    series_buf[:, 0:half] = flipped[:GAUGE_DEV]
    series_buf[:, half:2 * half] = flipped[GAUGE_DEV:]
    last = pltpu.make_async_copy(series_buf, series_out, out_sem.at[0, chunks])
    last.start()
    for d in range(1, n_gy):
        mail(d).wait_send()
    for copy in outs:
        copy.wait()
    last.wait()


def solution(mesh):
    n_gx, n_gy = mesh.shape["gx"], mesh.shape["gy"]

    def shards(surface, east_velocity, north_velocity, east_depth, north_depth, slot_gauge, slot_cell):
        rows, cols = surface.shape
        chunks = cols // LANES
        tall = rows + 2 * HALO
        plane = (chunks + 1) * tall
        half = 3 * STEPS // 2
        field = jax.ShapeDtypeStruct((rows, cols), jnp.float32)
        anywhere = pl.BlockSpec(memory_space=pl.ANY)
        dma = pltpu.SemaphoreType.DMA
        return pl.pallas_call(
            lambda *refs: kernel(n_gx, n_gy, *refs),
            name="window",
            out_shape=(field, field, field,
                       jax.ShapeDtypeStruct((GAUGE_DEV, 3 * STEPS), jnp.float32)),
            in_specs=[anywhere] * 5 + [pl.BlockSpec(memory_space=pltpu.VMEM),
                                       pl.BlockSpec(memory_space=pltpu.SMEM)],
            out_specs=(anywhere,) * 4,
            scratch_shapes=[
                pltpu.VMEM((5, chunks + 1, tall, LANES), jnp.float32),
                pltpu.VMEM((3 * (STEPS + 1) * plane, LANES), jnp.float32),
                pltpu.VMEM((2, rows, LANES), jnp.float32),
                pltpu.VMEM((2, tall, LANES), jnp.float32),
                pltpu.VMEM((chunks, rows, LANES), jnp.float32),
                pltpu.VMEM((n_gy, half, 2 * GAUGE_DEV), jnp.float32),
                pltpu.VMEM((n_gy, half, 2 * GAUGE_DEV), jnp.float32),
                pltpu.VMEM((GAUGE_DEV, 3 * STEPS), jnp.float32),
                dma((5, chunks)), dma((2,)), dma((2,)), dma((2,)), dma((2,)),
                dma((2,)), dma((2,)), dma((n_gy,)), dma((n_gy,)), dma((3, chunks + 1)),
            ],
            compiler_params=pltpu.CompilerParams(collective_id=0, has_side_effects=True,
                                                 vmem_limit_bytes=40 * 1024 * 1024),
        )(surface, east_velocity, north_velocity, east_depth, north_depth, slot_gauge, slot_cell)

    block = P("gx", "gy")
    lists = P(("gx", "gy"), None)
    return jax.shard_map(shards, mesh=mesh, in_specs=(block,) * 5 + (lists,) * 2,
                         out_specs=(block,) * 3 + (lists,), check_vma=False)
```

time: 285 us -> 39.2 us (0.14); the launches traced: 281 us -> 38.9 us
  starting transfers between devices: 159 us -> 0 us
  waiting for transfers between devices: 55.1 us -> 0 us
  matrix products: 32 us -> 0 us
  Pallas kernels: 0 us -> 29.8 us
  blocking collectives: 23.3 us -> 0 us
  other arithmetic: 4.07 us -> 0 us
    ppermute x64 -> x0, starting transfers between devices: 159 us -> none  [from_behind(): lax.ppermute(value, axis, [(source, source + steps) for source in range(f...]
    ppermute x64 -> x0, waiting for transfers between devices: 55.1 us -> none  [from_behind(): lax.ppermute(value, axis, [(source, source + steps) for source in range(f...]
    dot_general x49 -> x0, matrix products: 32 us -> none  [the longest x48 31 us: sample_cells(): rows_taken = jnp.dot(row_pick, field, precision=lax.Precision.HIGHEST)]
    pallas_call x0 -> x1, Pallas kernels: none -> 29.8 us  [shards(): pl.pallas_call(lambda *refs: kernel(n_gx, n_gy, *refs), name='window', ou...]
    all_gather x2 -> x0, blocking collectives: 23.3 us -> none  [the longest x1 14.1 us: shards(): lax.all_gather(slot_rows, 'gy', axis=0, tiled=True)]
    unnamed x20 -> x17, local copies, waits for them, and re-layouts: 1.79 us -> 7.79 us
    slice x96 -> x0, local copies, waits for them, and re-layouts: 3.08 us -> none  [the longest x16 1.44 us: update_velocity(): eta_right = jnp.concatenate([eta[:, 1:], right], 1)]
  transfers between devices with their start and end apart: 64 -> 0, of which waited for: 32 -> 0; matrix products, arithmetic and copies ran while one was open for 8% -> 0% of each run, Pallas kernels for 0% -> 0%
where the time goes in v1:
time: 39.2 us; the launch traced here: 38.9 us
  Pallas kernels  29.8 us (76%)
  local copies, waits for them, and re-layouts  8.47 us (22%)
  between operations  0.66 us (2%)
    pallas_call x1, Pallas kernels, shards(): pl.pallas_call(lambda *refs: kernel(n_gx, n_gy, *refs), name='window', ou...  29.8 us
    unnamed x17, local copies, waits for them, and re-layouts  7.79 us

profile of v1, /device:TPU:0, one launch (start us, length us, event | category | flops | bytes accessed | tf_op | source)
XLA Modules:
  0.0 38.9 jit_solution(7399076187337039824)
XLA Ops:
  0.6 0.0 copy-start
  0.6 0.9 %copy-done = f32[64,512]{1,0:T(8,128)S(1)} copy-done((f32[64,512]{1,0:T(8,128)S(1)}, f32[64,512]{1,0:T(8,128)}, u32[]{:S(2)}) %copy-start) | copy-done | bytes 131096
  1.5 0.0 copy-start.1
  1.5 0.9 %copy-done.1 = f32[64,512]{1,0:T(8,128)S(1)} copy-done((f32[64,512]{1,0:T(8,128)S(1)}, f32[64,512]{1,0:T(8,128)}, u32[]{:S(2)}) %copy-start.1) | copy-done | bytes 131096
  2.4 0.0 copy-start.2
  2.4 0.9 %copy-done.2 = f32[64,512]{1,0:T(8,128)S(1)} copy-done((f32[64,512]{1,0:T(8,128)S(1)}, f32[64,512]{1,0:T(8,128)}, u32[]{:S(2)}) %copy-start.2) | copy-done | bytes 131096
  3.3 0.0 copy-start.3
  3.4 0.9 %copy-done.3 = f32[64,512]{1,0:T(8,128)S(1)} copy-done((f32[64,512]{1,0:T(8,128)S(1)}, f32[64,512]{1,0:T(8,128)}, u32[]{:S(2)}) %copy-start.3) | copy-done | bytes 131096
  4.3 0.0 copy-start.4
  4.3 0.9 %copy-done.4 = f32[64,512]{1,0:T(8,128)S(1)} copy-done((f32[64,512]{1,0:T(8,128)S(1)}, f32[64,512]{1,0:T(8,128)}, u32[]{:S(2)}) %copy-start.4) | copy-done | bytes 131096
  5.2 0.0 copy-start.5
  5.2 0.7 %copy-done.5 = s32[1,128]{1,0:T(1,128)S(1)} copy-done((s32[1,128]{1,0:T(1,128)S(1)}, s32[1,128]{1,0:T(1,128)}, u32[]{:S(2)}) %copy-start.5) | copy-done | bytes 536
  5.8 0.0 copy-start.6
  5.8 0.7 %copy-done.6 = s32[1,128]{1,0:T(1,128)S(1)} copy-done((s32[1,128]{1,0:T(1,128)S(1)}, s32[1,128]{1,0:T(1,128)}, u32[]{:S(2)}) %copy-start.6) | copy-done | bytes 536
  6.5 29.8 %window.1 = (f32[64,512]{1,0:T(8,128)S(1)}, f32[64,512]{1,0:T(8,128)S(1)}, f32[64,512]{1,0:T(8,128)S(1)}, f32[64,48]{1,0:T(8,128)S(1)}) custom-call(f32[64,512]{1,0:T(8,128)S(1)} %copy-done, f32[64,512]{1,0:T(8,128)S(1)} %copy-done.1, f32[64,512]{1,0:T(8,128)S(1)} %copy-done.2, f32[64,512]{1,0:T(8,128)S(1)} %copy-done.3, f32[64,512]{1,0:T(8,128)S(1)} %copy-done.4, ...), custom_call_target="tpu_custom_call" | custom-call | tf_op jit(solution)/shard_map/window/pallas_call | solution.py:317
  36.3 0.7 %copy.11 = f32[64,48]{0,1:T(8,128)} copy(f32[64,48]{1,0:T(8,128)S(1)} %get-tuple-element.7) | data formatting | bytes 24576 | tf_op jit(solution)/shard_map/window/pallas_call | solution.py:317
  37.0 0.7 %copy.15 = f32[64,512]{1,0:T(8,128)} copy(f32[64,512]{1,0:T(8,128)S(1)} %get-tuple-element.12) | data formatting | bytes 262144
  37.6 0.7 %copy.16 = f32[64,512]{1,0:T(8,128)} copy(f32[64,512]{1,0:T(8,128)S(1)} %get-tuple-element.13) | data formatting | bytes 262144
  38.3 0.7 %copy.17 = f32[64,512]{1,0:T(8,128)} copy(f32[64,512]{1,0:T(8,128)S(1)} %get-tuple-element.14) | data formatting | bytes 262144
Async XLA Ops:
  0.6 0.9 %copy-start = (f32[64,512]{1,0:T(8,128)S(1)}, f32[64,512]{1,0:T(8,128)}, u32[]{:S(2)}) copy-start(f32[64,512]{1,0:T(8,128)} %refs_0_.1) | copy-start | bytes 393220
  1.5 0.9 %copy-start.1 = (f32[64,512]{1,0:T(8,128)S(1)}, f32[64,512]{1,0:T(8,128)}, u32[]{:S(2)}) copy-start(f32[64,512]{1,0:T(8,128)} %refs_1_.1) | copy-start | bytes 393220
  2.4 0.9 %copy-start.2 = (f32[64,512]{1,0:T(8,128)S(1)}, f32[64,512]{1,0:T(8,128)}, u32[]{:S(2)}) copy-start(f32[64,512]{1,0:T(8,128)} %refs_2_.1) | copy-start | bytes 393220
  3.3 0.9 %copy-start.3 = (f32[64,512]{1,0:T(8,128)S(1)}, f32[64,512]{1,0:T(8,128)}, u32[]{:S(2)}) copy-start(f32[64,512]{1,0:T(8,128)} %refs_3_.1) | copy-start | bytes 393220
  4.3 0.9 %copy-start.4 = (f32[64,512]{1,0:T(8,128)S(1)}, f32[64,512]{1,0:T(8,128)}, u32[]{:S(2)}) copy-start(f32[64,512]{1,0:T(8,128)} %refs_4_.1) | copy-start | bytes 393220
  5.2 0.7 %copy-start.5 = (s32[1,128]{1,0:T(1,128)S(1)}, s32[1,128]{1,0:T(1,128)}, u32[]{:S(2)}) copy-start(s32[1,128]{1,0:T(1,128)} %refs_5_.1) | copy-start | bytes 1540
  5.8 0.7 %copy-start.6 = (s32[1,128]{1,0:T(1,128)S(1)}, s32[1,128]{1,0:T(1,128)}, u32[]{:S(2)}) copy-start(s32[1,128]{1,0:T(1,128)} %refs_6_.1) | copy-start | bytes 1540

commit v2 on v1

--- a/solution.py
+++ b/solution.py
@@ -1,3 +1,5 @@
+import functools
+
 import jax
 import jax.numpy as jnp
 from jax import lax
@@ -14,16 +16,16 @@
 
 
 def kernel(
-    n_gx, n_gy, eta_hbm, east_hbm, north_hbm, hx_hbm, hy_hbm, ids_ref, cell_ref,
+    n_gx, n_gy, eta_hbm, east_hbm, north_hbm, hx_hbm, hy_hbm, ids_hbm, cell_hbm,
     eta_out, east_out, north_out, series_out,
-    wide, hist, packed, sides, final_eta, outbox, inbox, series_buf,
+    wide, hist, packed, sides, final_eta, outbox, inbox, series_buf, ids_ref, cell_ref,
     load_sem, row_send, row_recv, col_send, col_recv, corner_send, corner_recv,
-    mail_send, mail_recv, out_sem,
+    mail_send, mail_recv, out_sem, list_sem,
 ):
     rows, cols = eta_hbm.shape
     chunks = cols // LANES
     tall = rows + 2 * HALO
-    plane = (chunks + 1) * tall
+    plane = (chunks + 1) * tall + 1
     a, b = lax.axis_index("gx"), lax.axis_index("gy")
     has_up, has_down = a > 0, a < n_gx - 1
     has_left, has_right = b > 0, b < n_gy - 1
@@ -36,6 +38,10 @@
                 wide.at[f, c, HALO:HALO + rows, :], load_sem.at[f, c])
             copy.start()
             loads.append(copy)
+    for k, (src, dst) in enumerate(((ids_hbm, ids_ref), (cell_hbm, cell_ref))):
+        copy = pltpu.make_async_copy(src, dst, list_sem.at[k])
+        copy.start()
+        loads.append(copy)
 
     zero_rows = jnp.zeros((5, chunks, HALO, LANES), jnp.float32)
     zero_side = jnp.zeros((tall, LANES), jnp.float32)
@@ -180,49 +186,58 @@
 
     keep_row = has_down.astype(jnp.float32)
     keep_col = has_right.astype(jnp.float32)
+    sub = lax.broadcasted_iota(jnp.int32, (8, LANES), 0)
+    lane = lax.broadcasted_iota(jnp.int32, (8, LANES), 1)
     first_lane, last_lane = lane == 0, lane == LANES - 1
+    first_sub, last_sub = sub == 0, sub == 7
     side_mask = jnp.where(lane < LANES // 2, keep_col, 1.0)
-
-    def step(s, carry):
-        def at(f, c, t):
-            return pl.ds(pl.multiple_of((f * (STEPS + 1) + t) * plane + c * tall, 8), tall)
-
-        def put_eta(c, new):
-            base = pl.multiple_of((s + 1) * plane + c * tall, 8)
-            if c == chunks:
-                new = new * side_mask
-            hist[pl.ds(base, HALO + rows), :] = new[:HALO + rows]
-            hist[pl.ds(base + HALO + rows, HALO), :] = new[HALO + rows:] * keep_row
-
-        def rolled_eta(c):
-            return pltpu.roll(hist[at(0, c, s), :], LANES - 1, axis=1)
-
-        order = [chunks] + list(range(chunks))
-        rolled = rolled_eta(chunks)
-        held = None
-        behind = None
-        for c in order:
-            after = rolled_eta((c + 1) % (chunks + 1))
-            eta = hist[at(0, c, s), :]
-            east = hist[at(1, c, s), :] - (pltpu.roll(eta, tall - 1, axis=0) - eta)
-            north = hist[at(2, c, s), :] - (jnp.where(last_lane, after, rolled) - eta)
-            hist[at(1, c, s + 1), :] = east
-            hist[at(2, c, s + 1), :] = north
-            fx = wide[3, c] * east
-            fy = wide[4, c] * north
-            part = eta - (fx - pltpu.roll(fx, 1, axis=0)) - fy
-            moved = pltpu.roll(fy, 1, axis=1)
-            if c == chunks:
-                held = (part, moved)
-            else:
-                put_eta(c, part + jnp.where(first_lane, behind, moved))
-            behind = moved
-            rolled = after
-        part, moved = held
-        put_eta(chunks, part + jnp.where(first_lane, behind, moved))
+    every = range(chunks + 1)
+
+    def step(low, high, s, carry):
+        def at(f, c, t, block):
+            return pl.ds((f * (STEPS + 1) + t) * plane + c * tall + block * 8, 8)
+
+        def load_eta(block):
+            tiles = [hist[at(0, c, s, block), :] for c in every]
+            return tiles, [pltpu.roll(tile, 7, axis=0) for tile in tiles]
+
+        ahead = load_eta(low)
+        above = None
+        for block in range(low, high):
+            eta, lifted = ahead
+            ahead = load_eta(block + 1) if block + 1 < high else ahead
+            shifted = [pltpu.roll(tile, LANES - 1, axis=1) for tile in eta]
+            lowered, moved, part = [], [], []
+            for c in every:
+                down = jnp.where(last_sub, ahead[1][c], lifted[c])
+                right = jnp.where(last_lane, shifted[(c + 1) % (chunks + 1)], shifted[c])
+                east = hist[at(1, c, s, block), :] - (down - eta[c])
+                north = hist[at(2, c, s, block), :] - (right - eta[c])
+                hist[at(1, c, s + 1, block), :] = east
+                hist[at(2, c, s + 1, block), :] = north
+                fx = wide[3, c, block * 8:block * 8 + 8] * east
+                fy = wide[4, c, block * 8:block * 8 + 8] * north
+                lowered.append(pltpu.roll(fx, 1, axis=0))
+                moved.append(pltpu.roll(fy, 1, axis=1))
+                part.append(eta[c] - fx - fy)
+            if above is None:
+                above = lowered
+            for c in every:
+                up = jnp.where(first_sub, above[c], lowered[c])
+                left = jnp.where(first_lane, moved[c - 1], moved[c])
+                new = part[c] + up + left
+                if c == chunks:
+                    new = new * side_mask
+                if block * 8 >= HALO + rows:
+                    new = new * keep_row
+                hist[at(0, c, s + 1, block), :] = new
+            above = lowered
         return carry
 
-    lax.fori_loop(0, STEPS, step, 0)
+    blocks = tall // 8
+    lax.fori_loop(0, STEPS // 2, functools.partial(step, 0, blocks), 0)
+    trim = STEPS // 16
+    lax.fori_loop(STEPS // 2, STEPS, functools.partial(step, trim, blocks - trim), 0)
 
     outs = []
     for c in range(chunks):
@@ -242,12 +257,10 @@
 
     def pick(k, kept):
         cell = cell_ref[0, k]
-        row = cell // cols
-        col = cell - row * cols
-        chunk = col // LANES
-        here = col - chunk * LANES
+        row = lax.shift_right_logical(cell, cols.bit_length() - 1)
+        chunk = lax.shift_right_logical(cell, 7) & (chunks - 1)
         start = plane + chunk * tall + HALO + row
-        shift = lax.rem(k - here + LANES, LANES)
+        shift = (k - cell) & (LANES - 1)
         new = []
         for f in range(3):
             slab = hist[pl.ds(f * (STEPS + 1) * plane + start, STEPS, stride=plane), :]
@@ -290,9 +303,8 @@
     for d in range(1, n_gy):
         mail(d).wait_recv()
         total = total + inbox[d]
-    flipped = total.T
-    series_buf[:, 0:half] = flipped[:GAUGE_DEV]
-    series_buf[:, half:2 * half] = flipped[GAUGE_DEV:]
+    series_buf[0:half, :] = total[:, :GAUGE_DEV]
+    series_buf[half:2 * half, :] = pltpu.roll(total, GAUGE_DEV, axis=1)[:, :GAUGE_DEV]
     last = pltpu.make_async_copy(series_buf, series_out, out_sem.at[0, chunks])
     last.start()
     for d in range(1, n_gy):
@@ -302,6 +314,15 @@
     last.wait()
 
 
+def flush(*refs):
+    sem = refs[8]
+    copies = [pltpu.make_async_copy(refs[k], refs[4 + k], sem.at[k]) for k in range(4)]
+    for copy in copies:
+        copy.start()
+    for copy in copies:
+        copy.wait()
+
+
 def solution(mesh):
     n_gx, n_gy = mesh.shape["gx"], mesh.shape["gy"]
 
@@ -309,18 +330,21 @@
         rows, cols = surface.shape
         chunks = cols // LANES
         tall = rows + 2 * HALO
-        plane = (chunks + 1) * tall
+        plane = (chunks + 1) * tall + 1
         half = 3 * STEPS // 2
         field = jax.ShapeDtypeStruct((rows, cols), jnp.float32)
         anywhere = pl.BlockSpec(memory_space=pl.ANY)
+        in_hbm = pl.BlockSpec(memory_space=pltpu.HBM)
+        near = pltpu.VMEM((rows, cols), jnp.float32)
+        in_vmem = pl.BlockSpec(memory_space=pltpu.VMEM)
+        series = jax.ShapeDtypeStruct((3 * STEPS, GAUGE_DEV), jnp.float32)
+        slots = slot_gauge.shape[1]
         dma = pltpu.SemaphoreType.DMA
-        return pl.pallas_call(
+        results = pl.pallas_call(
             lambda *refs: kernel(n_gx, n_gy, *refs),
             name="window",
-            out_shape=(field, field, field,
-                       jax.ShapeDtypeStruct((GAUGE_DEV, 3 * STEPS), jnp.float32)),
-            in_specs=[anywhere] * 5 + [pl.BlockSpec(memory_space=pltpu.VMEM),
-                                       pl.BlockSpec(memory_space=pltpu.SMEM)],
+            out_shape=(near, near, near, pltpu.VMEM(series.shape, series.dtype)),
+            in_specs=[in_hbm] * 7,
             out_specs=(anywhere,) * 4,
             scratch_shapes=[
                 pltpu.VMEM((5, chunks + 1, tall, LANES), jnp.float32),
@@ -330,13 +354,21 @@
                 pltpu.VMEM((chunks, rows, LANES), jnp.float32),
                 pltpu.VMEM((n_gy, half, 2 * GAUGE_DEV), jnp.float32),
                 pltpu.VMEM((n_gy, half, 2 * GAUGE_DEV), jnp.float32),
-                pltpu.VMEM((GAUGE_DEV, 3 * STEPS), jnp.float32),
+                pltpu.VMEM((3 * STEPS, GAUGE_DEV), jnp.float32),
+                pltpu.VMEM((1, slots), jnp.int32), pltpu.SMEM((1, slots), jnp.int32),
                 dma((5, chunks)), dma((2,)), dma((2,)), dma((2,)), dma((2,)),
-                dma((2,)), dma((2,)), dma((n_gy,)), dma((n_gy,)), dma((3, chunks + 1)),
+                dma((2,)), dma((2,)), dma((n_gy,)), dma((n_gy,)), dma((3, chunks + 1)), dma((2,)),
             ],
             compiler_params=pltpu.CompilerParams(collective_id=0, has_side_effects=True,
                                                  vmem_limit_bytes=40 * 1024 * 1024),
-        )(surface, east_velocity, north_velocity, east_depth, north_depth, slot_gauge, slot_cell)
+        )(*[pltpu.with_memory_space_constraint(x, pltpu.HBM) for x in (
+            surface, east_velocity, north_velocity, east_depth, north_depth, slot_gauge, slot_cell)])
+        eta, east, north, gauges = pl.pallas_call(
+            flush, name="flush", out_shape=(field, field, field, series),
+            in_specs=[in_vmem] * 4, out_specs=(in_hbm,) * 4,
+            scratch_shapes=[dma((4,))],
+        )(*[pltpu.with_memory_space_constraint(x, pltpu.VMEM) for x in results])
+        return eta, east, north, gauges.T
 
     block = P("gx", "gy")
     lists = P(("gx", "gy"), None)

time: 39.2 us -> 27.1 us (0.69)
  local copies, waits for them, and re-layouts: 8.47 us -> 0 us
  Pallas kernels: 29.8 us -> 26.3 us
    unnamed x17 -> x0, local copies, waits for them, and re-layouts: 7.79 us -> none
    pallas_call x1, Pallas kernels: 29.8 us -> 25.5 us  [shards(): pl.pallas_call(lambda *refs: kernel(n_gx, n_gy, *refs), name='window', ou...]
    pallas_call x0 -> x1, Pallas kernels: none -> 0.78 us  [shards(): pl.pallas_call(flush, name='flush', out_shape=(field, field, field, serie...]
    pallas_call x1 -> x0, local copies, waits for them, and re-layouts: 0.69 us -> none  [shards(): pl.pallas_call(lambda *refs: kernel(n_gx, n_gy, *refs), name='window', ou...]
where the time goes in v2:
time: 27.1 us; the launch traced here: 26.9 us
  Pallas kernels  26.3 us (97%)
  between operations  0.64 us (2%)
    pallas_call x1, Pallas kernels, shards(): pl.pallas_call(lambda *refs: kernel(n_gx, n_gy, *refs), name='window', ou...  25.5 us
    pallas_call x1, Pallas kernels, shards(): pl.pallas_call(flush, name='flush', out_shape=(field, field, field, serie...  0.78 us

profile of v2, /device:TPU:0, one launch (start us, length us, event | category | flops | bytes accessed | tf_op | source)
XLA Modules:
  0.0 26.9 jit_solution(12380405217939836463)
XLA Ops:
  0.6 25.5 %window.1 = (f32[64,512]{1,0:T(8,128)S(1)}, f32[64,512]{1,0:T(8,128)S(1)}, f32[64,512]{1,0:T(8,128)S(1)}, f32[48,64]{1,0:T(8,128)S(1)}) custom-call(f32[64,512]{1,0:T(8,128)} %refs_0_.1, f32[64,512]{1,0:T(8,128)} %refs_1_.1, f32[64,512]{1,0:T(8,128)} %refs_2_.1, f32[64,512]{1,0:T(8,128)} %refs_3_.1, f32[64,512]{1,0:T(8,128)} %refs_4_.1, s32[1,128]{1,0:T(1,128)} %refs_5_.1, ...), custom_call_target="tpu_custom_call" | custom-call | tf_op jit(solution)/shard_map/window/pallas_call | solution.py:343
  26.2 0.8 %flush.1 = (f32[64,512]{1,0:T(8,128)}, f32[64,512]{1,0:T(8,128)}, f32[64,512]{1,0:T(8,128)}, f32[48,64]{1,0:T(8,128)}) custom-call(f32[64,512]{1,0:T(8,128)S(1)} %get-tuple-element.12.refs_0_, f32[64,512]{1,0:T(8,128)S(1)} %get-tuple-element.13.refs_1_, f32[64,512]{1,0:T(8,128)S(1)} %get-tuple-element.14.refs_2_, f32[48,64]{1,0:T(8,128)S(1)} %get-tuple-element.15.refs_3_), custom_call_target="tpu_custom_call" | custom-call | tf_op jit(solution)/shard_map/flush/pallas_call | solution.py:366

commit v3 on v2

--- a/solution.py
+++ b/solution.py
@@ -18,7 +18,7 @@
 def kernel(
     n_gx, n_gy, eta_hbm, east_hbm, north_hbm, hx_hbm, hy_hbm, ids_hbm, cell_hbm,
     eta_out, east_out, north_out, series_out,
-    wide, hist, packed, sides, final_eta, outbox, inbox, series_buf, ids_ref, cell_ref,
+    wide, coef, hist, packed, sides, final_eta, outbox, inbox, series_buf, ids_ref, cell_ref,
     load_sem, row_send, row_recv, col_send, col_recv, corner_send, corner_recv,
     mail_send, mail_recv, out_sem, list_sem,
 ):
@@ -49,12 +49,12 @@
 
     @pl.when(jnp.logical_not(has_up))
     def _():
-        wide[:, 0:chunks, 0:HALO, :] = zero_rows
+        wide[:, :, 0:HALO, :] = zero_rows
         sides[:, 0:HALO, :] = zero_cap
 
     @pl.when(jnp.logical_not(has_down))
     def _():
-        wide[:, 0:chunks, HALO + rows:tall, :] = zero_rows
+        wide[:, :, HALO + rows:tall, :] = zero_rows
         sides[:, HALO + rows:tall, :] = zero_cap
 
     @pl.when(jnp.logical_not(has_left))
@@ -87,8 +87,8 @@
         source = (HALO, rows)[k]
         target = (HALO + rows, 0)[k]
         return pltpu.make_async_remote_copy(
-            wide.at[:, 0:chunks, source:source + HALO, :],
-            wide.at[:, 0:chunks, target:target + HALO, :],
+            wide.at[:, :, source:source + HALO, :],
+            wide.at[:, :, target:target + HALO, :],
             row_send.at[k], row_recv.at[k],
             device_id=(a + (-1, 1)[k], b), device_id_type=MESH)
 
@@ -105,6 +105,14 @@
             packed.at[k], sides.at[k, HALO:HALO + rows, :],
             col_send.at[k], col_recv.at[k],
             device_id=(a, b + (1, -1)[k]), device_id_type=MESH)
+
+    @pl.when(has_up)
+    def _():
+        row_copy(0).start()
+
+    @pl.when(has_down)
+    def _():
+        row_copy(1).start()
 
     lane = lax.broadcasted_iota(jnp.int32, (rows, LANES), 1)
     for k in range(2):
@@ -124,14 +132,6 @@
     def _():
         col_copy(1).start()
 
-    @pl.when(has_up)
-    def _():
-        row_copy(0).start()
-
-    @pl.when(has_down)
-    def _():
-        row_copy(1).start()
-
     @pl.when(has_right)
     def _():
         col_copy(0).wait_send()
@@ -150,39 +150,27 @@
     def _():
         corner_copy(1).start()
 
-    @pl.when(has_up)
-    def _():
-        row_copy(0).wait_send()
-        row_copy(1).wait_recv()
-        corner_copy(0).wait_send()
-        corner_copy(1).wait_recv()
-
-    @pl.when(has_down)
-    def _():
-        row_copy(1).wait_send()
-        row_copy(0).wait_recv()
-        corner_copy(1).wait_send()
-        corner_copy(0).wait_recv()
-
-    lane = lax.broadcasted_iota(jnp.int32, (tall, LANES), 1)
     scales = (time_step, 1.0, 1.0, time_step * time_step, time_step * time_step)
-    for f in range(5):
-        for c in range(chunks + 1):
-            if c < chunks:
-                tile = wide[f, c]
-            else:
-                left, right = sides[0], sides[1]
-                left = pltpu.roll(left, (LANES - HALO - f * HALO) % LANES, axis=1)
-                if f:
-                    right = pltpu.roll(right, (LANES - f * HALO) % LANES, axis=1)
-                tile = jnp.where(lane < HALO, right, jnp.where(lane >= LANES - HALO, left, 0.0))
-            if f in (0, 3, 4):
-                tile = tile * scales[f]
-            if f < 3:
-                start = f * (STEPS + 1) * plane + c * tall
-                hist[start:start + tall, :] = tile
-            else:
-                wide[f, c] = tile
+
+    def prepare(low, high):
+        lane = lax.broadcasted_iota(jnp.int32, (high - low, LANES), 1)
+        for f in range(5):
+            for c in range(chunks + 1):
+                if c < chunks:
+                    tile = wide[f, c, low:high]
+                else:
+                    left, right = sides[0, low:high], sides[1, low:high]
+                    left = pltpu.roll(left, (LANES - HALO - f * HALO) % LANES, axis=1)
+                    if f:
+                        right = pltpu.roll(right, (LANES - f * HALO) % LANES, axis=1)
+                    tile = jnp.where(lane < HALO, right, jnp.where(lane >= LANES - HALO, left, 0.0))
+                if f in (0, 3, 4):
+                    tile = tile * scales[f]
+                if f < 3:
+                    start = f * (STEPS + 1) * plane + c * tall + low
+                    hist[start:start + high - low, :] = tile
+                else:
+                    coef[f - 3, c, low:high] = tile
 
     keep_row = has_down.astype(jnp.float32)
     keep_col = has_right.astype(jnp.float32)
@@ -193,7 +181,7 @@
     side_mask = jnp.where(lane < LANES // 2, keep_col, 1.0)
     every = range(chunks + 1)
 
-    def step(low, high, s, carry):
+    def sweep(s, low, high, exact_above=False, exact_ahead=False):
         def at(f, c, t, block):
             return pl.ds((f * (STEPS + 1) + t) * plane + c * tall + block * 8, 8)
 
@@ -203,9 +191,14 @@
 
         ahead = load_eta(low)
         above = None
+        if exact_above:
+            above = [
+                pltpu.roll(coef[0, c, low * 8 - 8:low * 8] * hist[at(1, c, s + 1, low - 1), :], 1, axis=0)
+                for c in every]
         for block in range(low, high):
             eta, lifted = ahead
-            ahead = load_eta(block + 1) if block + 1 < high else ahead
+            if block + 1 < high or exact_ahead:
+                ahead = load_eta(block + 1)
             shifted = [pltpu.roll(tile, LANES - 1, axis=1) for tile in eta]
             lowered, moved, part = [], [], []
             for c in every:
@@ -215,8 +208,8 @@
                 north = hist[at(2, c, s, block), :] - (right - eta[c])
                 hist[at(1, c, s + 1, block), :] = east
                 hist[at(2, c, s + 1, block), :] = north
-                fx = wide[3, c, block * 8:block * 8 + 8] * east
-                fy = wide[4, c, block * 8:block * 8 + 8] * north
+                fx = coef[0, c, block * 8:block * 8 + 8] * east
+                fy = coef[1, c, block * 8:block * 8 + 8] * north
                 lowered.append(pltpu.roll(fx, 1, axis=0))
                 moved.append(pltpu.roll(fy, 1, axis=1))
                 part.append(eta[c] - fx - fy)
@@ -232,12 +225,51 @@
                     new = new * keep_row
                 hist[at(0, c, s + 1, block), :] = new
             above = lowered
+
+    first, last = HALO // 8, (HALO + rows) // 8
+    half_halo = first // 2
+    middle_step = STEPS // 2
+
+    def core_early(s, carry):
+        sweep(s, first, last)
         return carry
 
-    blocks = tall // 8
-    lax.fori_loop(0, STEPS // 2, functools.partial(step, 0, blocks), 0)
-    trim = STEPS // 16
-    lax.fori_loop(STEPS // 2, STEPS, functools.partial(step, trim, blocks - trim), 0)
+    def core_late(s, carry):
+        sweep(s, first + half_halo, last - half_halo)
+        return carry
+
+    def rim_early(s, carry):
+        sweep(s, 0, first + half_halo, exact_ahead=True)
+        sweep(s, last - half_halo, last + first, exact_above=True)
+        return carry
+
+    def rim_late(s, carry):
+        sweep(s, half_halo, first + 2 * half_halo, exact_ahead=True)
+        sweep(s, last - 2 * half_halo, last + half_halo, exact_above=True)
+        return carry
+
+    prepare(HALO, HALO + rows)
+    lax.fori_loop(0, middle_step, core_early, 0)
+    lax.fori_loop(middle_step, STEPS, core_late, 0)
+
+    @pl.when(has_up)
+    def _():
+        row_copy(0).wait_send()
+        row_copy(1).wait_recv()
+        corner_copy(0).wait_send()
+        corner_copy(1).wait_recv()
+
+    @pl.when(has_down)
+    def _():
+        row_copy(1).wait_send()
+        row_copy(0).wait_recv()
+        corner_copy(1).wait_send()
+        corner_copy(0).wait_recv()
+
+    prepare(0, HALO)
+    prepare(HALO + rows, tall)
+    lax.fori_loop(0, middle_step, rim_early, 0)
+    lax.fori_loop(middle_step, STEPS, rim_late, 0)
 
     outs = []
     for c in range(chunks):
@@ -269,7 +301,7 @@
         return tuple(new)
 
     blank = jnp.zeros((STEPS, slots), jnp.float32)
-    kept = lax.fori_loop(0, slots, pick, (blank, blank, blank), unroll=8)
+    kept = lax.fori_loop(0, slots, pick, (blank, blank, blank), unroll=16)
     records = jnp.concatenate([kept[0] * (1.0 / time_step), kept[1], kept[2]], 0)
     half = 3 * STEPS // 2
     pair = jnp.concatenate([records[:half], records[half:]], 1)
@@ -305,13 +337,13 @@
         total = total + inbox[d]
     series_buf[0:half, :] = total[:, :GAUGE_DEV]
     series_buf[half:2 * half, :] = pltpu.roll(total, GAUGE_DEV, axis=1)[:, :GAUGE_DEV]
-    last = pltpu.make_async_copy(series_buf, series_out, out_sem.at[0, chunks])
-    last.start()
+    final = pltpu.make_async_copy(series_buf, series_out, out_sem.at[0, chunks])
+    final.start()
     for d in range(1, n_gy):
         mail(d).wait_send()
     for copy in outs:
         copy.wait()
-    last.wait()
+    final.wait()
 
 
 def flush(*refs):
@@ -347,7 +379,8 @@
             in_specs=[in_hbm] * 7,
             out_specs=(anywhere,) * 4,
             scratch_shapes=[
-                pltpu.VMEM((5, chunks + 1, tall, LANES), jnp.float32),
+                pltpu.VMEM((5, chunks, tall, LANES), jnp.float32),
+                pltpu.VMEM((2, chunks + 1, tall, LANES), jnp.float32),
                 pltpu.VMEM((3 * (STEPS + 1) * plane, LANES), jnp.float32),
                 pltpu.VMEM((2, rows, LANES), jnp.float32),
                 pltpu.VMEM((2, tall, LANES), jnp.float32),

time: 27.1 us -> 25.4 us (0.937)
  Pallas kernels: 26.3 us -> 24.6 us
    pallas_call x1, Pallas kernels: 25.5 us -> 23.8 us  [shards(): pl.pallas_call(lambda *refs: kernel(n_gx, n_gy, *refs), name='window', ou...]
where the time goes in v3:
time: 25.4 us; the launch traced here: 25.2 us
  Pallas kernels  24.6 us (97%)
  between operations  0.64 us (3%)
    pallas_call x1, Pallas kernels, shards(): pl.pallas_call(lambda *refs: kernel(n_gx, n_gy, *refs), name='window', ou...  23.8 us
    pallas_call x1, Pallas kernels, shards(): pl.pallas_call(flush, name='flush', out_shape=(field, field, field, serie...  0.78 us

profile of v3, /device:TPU:0, one launch (start us, length us, event | category | flops | bytes accessed | tf_op | source)
XLA Modules:
  0.0 25.2 jit_solution(18183228097575903448)
XLA Ops:
  0.6 23.8 %window.1 = (f32[64,512]{1,0:T(8,128)S(1)}, f32[64,512]{1,0:T(8,128)S(1)}, f32[64,512]{1,0:T(8,128)S(1)}, f32[48,64]{1,0:T(8,128)S(1)}) custom-call(f32[64,512]{1,0:T(8,128)} %refs_0_.1, f32[64,512]{1,0:T(8,128)} %refs_1_.1, f32[64,512]{1,0:T(8,128)} %refs_2_.1, f32[64,512]{1,0:T(8,128)} %refs_3_.1, f32[64,512]{1,0:T(8,128)} %refs_4_.1, s32[1,128]{1,0:T(1,128)} %refs_5_.1, ...), custom_call_target="tpu_custom_call" | custom-call | tf_op jit(solution)/shard_map/window/pallas_call | solution.py:375
  24.4 0.8 %flush.1 = (f32[64,512]{1,0:T(8,128)}, f32[64,512]{1,0:T(8,128)}, f32[64,512]{1,0:T(8,128)}, f32[48,64]{1,0:T(8,128)}) custom-call(f32[64,512]{1,0:T(8,128)S(1)} %get-tuple-element.12.refs_0_, f32[64,512]{1,0:T(8,128)S(1)} %get-tuple-element.13.refs_1_, f32[64,512]{1,0:T(8,128)S(1)} %get-tuple-element.14.refs_2_, f32[48,64]{1,0:T(8,128)S(1)} %get-tuple-element.15.refs_3_), custom_call_target="tpu_custom_call" | custom-call | tf_op jit(solution)/shard_map/flush/pallas_call | solution.py:399

commit v4 on v3

--- a/solution.py
+++ b/solution.py
@@ -18,7 +18,7 @@
 def kernel(
     n_gx, n_gy, eta_hbm, east_hbm, north_hbm, hx_hbm, hy_hbm, ids_hbm, cell_hbm,
     eta_out, east_out, north_out, series_out,
-    wide, coef, hist, packed, sides, final_eta, outbox, inbox, series_buf, ids_ref, cell_ref,
+    wide, coef, hist, packed, sides, final_eta, outbox, inbox, chooser, series_buf, ids_ref, cell_ref,
     load_sem, row_send, row_recv, col_send, col_recv, corner_send, corner_recv,
     mail_send, mail_recv, out_sem, list_sem,
 ):
@@ -59,11 +59,11 @@
 
     @pl.when(jnp.logical_not(has_left))
     def _():
-        sides[0, HALO:HALO + rows, :] = zero_side[:rows]
+        sides[0] = zero_side
 
     @pl.when(jnp.logical_not(has_right))
     def _():
-        sides[1, HALO:HALO + rows, :] = zero_side[:rows]
+        sides[1] = zero_side
 
     barrier = pltpu.get_barrier_semaphore()
 
@@ -74,11 +74,26 @@
     @pl.when(has_down)
     def _():
         pl.semaphore_signal(barrier, inc=1, device_id=(a + 1, b), device_id_type=MESH)
+
+    diagonals = [(v, k) for v in range(2) for k in range(2)]
+
+    def toward(v, k):
+        return jnp.logical_and((has_up, has_down)[v], (has_right, has_left)[k])
+
+    for v, k in diagonals:
+        @pl.when(toward(v, k))
+        def _():
+            pl.semaphore_signal(
+                barrier, inc=1, device_id=(a + (-1, 1)[v], b + (1, -1)[k]), device_id_type=MESH)
 
     for d in range(1, n_gy):
         pl.semaphore_signal(barrier, inc=1, device_id=(a, lax.rem(b + d, n_gy)), device_id_type=MESH)
+    def flag(test):
+        return test.astype(jnp.int32)
+
+    across = flag(has_up) + flag(has_down)
     pl.semaphore_wait(
-        barrier, n_gy - 1 + has_up.astype(jnp.int32) + has_down.astype(jnp.int32))
+        barrier, n_gy - 1 + across + across * (flag(has_left) + flag(has_right)))
 
     for copy in loads:
         copy.wait()
@@ -92,27 +107,19 @@
             row_send.at[k], row_recv.at[k],
             device_id=(a + (-1, 1)[k], b), device_id_type=MESH)
 
-    def corner_copy(k):
-        source = (HALO, rows)[k]
-        target = (HALO + rows, 0)[k]
+    def corner_copy(v, k):
+        source = (0, rows - HALO)[v]
+        target = (HALO + rows, 0)[v]
         return pltpu.make_async_remote_copy(
-            sides.at[:, source:source + HALO, :], sides.at[:, target:target + HALO, :],
-            corner_send.at[k], corner_recv.at[k],
-            device_id=(a + (-1, 1)[k], b), device_id_type=MESH)
+            packed.at[k, source:source + HALO, :], sides.at[k, target:target + HALO, :],
+            corner_send.at[v, k], corner_recv.at[v, k],
+            device_id=(a + (-1, 1)[v], b + (1, -1)[k]), device_id_type=MESH)
 
     def col_copy(k):
         return pltpu.make_async_remote_copy(
             packed.at[k], sides.at[k, HALO:HALO + rows, :],
             col_send.at[k], col_recv.at[k],
             device_id=(a, b + (1, -1)[k]), device_id_type=MESH)
-
-    @pl.when(has_up)
-    def _():
-        row_copy(0).start()
-
-    @pl.when(has_down)
-    def _():
-        row_copy(1).start()
 
     lane = lax.broadcasted_iota(jnp.int32, (rows, LANES), 1)
     for k in range(2):
@@ -132,6 +139,19 @@
     def _():
         col_copy(1).start()
 
+    for v, k in diagonals:
+        @pl.when(toward(v, k))
+        def _():
+            corner_copy(v, k).start()
+
+    @pl.when(has_up)
+    def _():
+        row_copy(0).start()
+
+    @pl.when(has_down)
+    def _():
+        row_copy(1).start()
+
     @pl.when(has_right)
     def _():
         col_copy(0).wait_send()
@@ -141,14 +161,6 @@
     def _():
         col_copy(1).wait_send()
         col_copy(0).wait_recv()
-
-    @pl.when(has_up)
-    def _():
-        corner_copy(0).start()
-
-    @pl.when(has_down)
-    def _():
-        corner_copy(1).start()
 
     scales = (time_step, 1.0, 1.0, time_step * time_step, time_step * time_step)
 
@@ -252,24 +264,76 @@
     lax.fori_loop(0, middle_step, core_early, 0)
     lax.fori_loop(middle_step, STEPS, core_late, 0)
 
+    slots = ids_ref.shape[1]
+    local_ids = ids_ref[...] - a * (n_gy * GAUGE_DEV)
+    entry = lax.broadcasted_iota(jnp.int32, (2 * GAUGE_DEV, slots), 0)
+    for o in range(n_gy):
+        lower = (entry < GAUGE_DEV) & (local_ids == entry + o * GAUGE_DEV)
+        upper = (entry >= GAUGE_DEV) & (local_ids == entry + (o - 1) * GAUGE_DEV)
+        chooser[o] = jnp.concatenate(
+            [jnp.where(lower, 1.0, 0.0), jnp.where(upper, 1.0, 0.0)], 1).astype(jnp.bfloat16)
+
     @pl.when(has_up)
     def _():
         row_copy(0).wait_send()
         row_copy(1).wait_recv()
-        corner_copy(0).wait_send()
-        corner_copy(1).wait_recv()
 
     @pl.when(has_down)
     def _():
         row_copy(1).wait_send()
         row_copy(0).wait_recv()
-        corner_copy(1).wait_send()
-        corner_copy(0).wait_recv()
+
+    for v, k in diagonals:
+        @pl.when(toward(v, k))
+        def _():
+            corner_copy(v, k).wait_send()
+            corner_copy(1 - v, 1 - k).wait_recv()
 
     prepare(0, HALO)
     prepare(HALO + rows, tall)
     lax.fori_loop(0, middle_step, rim_early, 0)
     lax.fori_loop(middle_step, STEPS, rim_late, 0)
+
+    slot_lane = lax.broadcasted_iota(jnp.int32, (STEPS, slots), 1)
+
+    def pick(k, kept):
+        cell = cell_ref[0, k]
+        row = lax.shift_right_logical(cell, cols.bit_length() - 1)
+        chunk = lax.shift_right_logical(cell, 7) & (chunks - 1)
+        start = plane + chunk * tall + HALO + row
+        shift = (k - cell) & (LANES - 1)
+        new = []
+        for f in range(3):
+            slab = hist[pl.ds(f * (STEPS + 1) * plane + start, STEPS, stride=plane), :]
+            slab = pltpu.roll(slab, shift, axis=1)
+            new.append(jnp.where(slot_lane == k, slab, kept[f]))
+        return tuple(new)
+
+    blank = jnp.zeros((STEPS, slots), jnp.float32)
+    kept = lax.fori_loop(0, slots, pick, (blank, blank, blank), unroll=16)
+    records = jnp.concatenate([kept[0] * (1.0 / time_step), kept[1], kept[2]], 0)
+    half = 3 * STEPS // 2
+    pair = jnp.concatenate([records[:half], records[half:]], 1)
+    high = pair.astype(jnp.bfloat16)
+    rest = pair - high.astype(jnp.float32)
+    middle = rest.astype(jnp.bfloat16)
+    low = (rest - middle.astype(jnp.float32)).astype(jnp.bfloat16)
+    for o in range(n_gy):
+        total = None
+        for piece in (low, middle, high):
+            got = lax.dot_general(piece, chooser[o], (((1,), (1,)), ((), ())),
+                                  preferred_element_type=jnp.float32)
+            total = got if total is None else total + got
+        outbox[o] = total
+
+    def mail(d):
+        peer = lax.rem(b + d, n_gy)
+        return pltpu.make_async_remote_copy(
+            outbox.at[peer], inbox.at[d], mail_send.at[d], mail_recv.at[d],
+            device_id=(a, peer), device_id_type=MESH)
+
+    for d in range(1, n_gy):
+        mail(d).start()
 
     outs = []
     for c in range(chunks):
@@ -284,53 +348,6 @@
     for copy in outs:
         copy.start()
 
-    slots = ids_ref.shape[1]
-    slot_lane = lax.broadcasted_iota(jnp.int32, (STEPS, slots), 1)
-
-    def pick(k, kept):
-        cell = cell_ref[0, k]
-        row = lax.shift_right_logical(cell, cols.bit_length() - 1)
-        chunk = lax.shift_right_logical(cell, 7) & (chunks - 1)
-        start = plane + chunk * tall + HALO + row
-        shift = (k - cell) & (LANES - 1)
-        new = []
-        for f in range(3):
-            slab = hist[pl.ds(f * (STEPS + 1) * plane + start, STEPS, stride=plane), :]
-            slab = pltpu.roll(slab, shift, axis=1)
-            new.append(jnp.where(slot_lane == k, slab, kept[f]))
-        return tuple(new)
-
-    blank = jnp.zeros((STEPS, slots), jnp.float32)
-    kept = lax.fori_loop(0, slots, pick, (blank, blank, blank), unroll=16)
-    records = jnp.concatenate([kept[0] * (1.0 / time_step), kept[1], kept[2]], 0)
-    half = 3 * STEPS // 2
-    pair = jnp.concatenate([records[:half], records[half:]], 1)
-    high = pair.astype(jnp.bfloat16)
-    rest = pair - high.astype(jnp.float32)
-    middle = rest.astype(jnp.bfloat16)
-    low = (rest - middle.astype(jnp.float32)).astype(jnp.bfloat16)
-    local_ids = ids_ref[...] - a * (n_gy * GAUGE_DEV)
-    entry = lax.broadcasted_iota(jnp.int32, (2 * GAUGE_DEV, slots), 0)
-    for o in range(n_gy):
-        lower = (entry < GAUGE_DEV) & (local_ids == entry + o * GAUGE_DEV)
-        upper = (entry >= GAUGE_DEV) & (local_ids == entry + (o - 1) * GAUGE_DEV)
-        chooser = jnp.concatenate(
-            [jnp.where(lower, 1.0, 0.0), jnp.where(upper, 1.0, 0.0)], 1).astype(jnp.bfloat16)
-        total = None
-        for piece in (low, middle, high):
-            got = lax.dot_general(piece, chooser, (((1,), (1,)), ((), ())),
-                                  preferred_element_type=jnp.float32)
-            total = got if total is None else total + got
-        outbox[o] = total
-
-    def mail(d):
-        peer = lax.rem(b + d, n_gy)
-        return pltpu.make_async_remote_copy(
-            outbox.at[peer], inbox.at[d], mail_send.at[d], mail_recv.at[d],
-            device_id=(a, peer), device_id_type=MESH)
-
-    for d in range(1, n_gy):
-        mail(d).start()
     total = outbox[b]
     for d in range(1, n_gy):
         mail(d).wait_recv()
@@ -387,10 +404,11 @@
                 pltpu.VMEM((chunks, rows, LANES), jnp.float32),
                 pltpu.VMEM((n_gy, half, 2 * GAUGE_DEV), jnp.float32),
                 pltpu.VMEM((n_gy, half, 2 * GAUGE_DEV), jnp.float32),
+                pltpu.VMEM((n_gy, 2 * GAUGE_DEV, 2 * slots), jnp.bfloat16),
                 pltpu.VMEM((3 * STEPS, GAUGE_DEV), jnp.float32),
                 pltpu.VMEM((1, slots), jnp.int32), pltpu.SMEM((1, slots), jnp.int32),
                 dma((5, chunks)), dma((2,)), dma((2,)), dma((2,)), dma((2,)),
-                dma((2,)), dma((2,)), dma((n_gy,)), dma((n_gy,)), dma((3, chunks + 1)), dma((2,)),
+                dma((2, 2)), dma((2, 2)), dma((n_gy,)), dma((n_gy,)), dma((3, chunks + 1)), dma((2,)),
             ],
             compiler_params=pltpu.CompilerParams(collective_id=0, has_side_effects=True,
                                                  vmem_limit_bytes=40 * 1024 * 1024),

time: 25.4 us -> 25 us (0.984)
  the two profiles are of different devices: /device:TPU:0 before, /device:TPU:5 now
where the time goes in v4:
time: 25 us; the launch traced here: 24.8 us
  Pallas kernels  24.2 us (97%)
  between operations  0.64 us (3%)
    pallas_call x1, Pallas kernels, shards(): pl.pallas_call(lambda *refs: kernel(n_gx, n_gy, *refs), name='window', ou...  23.4 us
    pallas_call x1, Pallas kernels, shards(): pl.pallas_call(flush, name='flush', out_shape=(field, field, field, serie...  0.78 us

profile of v4, /device:TPU:5, one launch (start us, length us, event | category | flops | bytes accessed | tf_op | source)
XLA Modules:
  0.0 24.8 jit_solution(12707786517727218777)
XLA Ops:
  0.6 23.4 %window.1 = (f32[64,512]{1,0:T(8,128)S(1)}, f32[64,512]{1,0:T(8,128)S(1)}, f32[64,512]{1,0:T(8,128)S(1)}, f32[48,64]{1,0:T(8,128)S(1)}) custom-call(f32[64,512]{1,0:T(8,128)} %refs_0_.1, f32[64,512]{1,0:T(8,128)} %refs_1_.1, f32[64,512]{1,0:T(8,128)} %refs_2_.1, f32[64,512]{1,0:T(8,128)} %refs_3_.1, f32[64,512]{1,0:T(8,128)} %refs_4_.1, s32[1,128]{1,0:T(1,128)} %refs_5_.1, ...), custom_call_target="tpu_custom_call" | custom-call | tf_op jit(solution)/shard_map/window/pallas_call | solution.py:392
  24.0 0.8 %flush.1 = (f32[64,512]{1,0:T(8,128)}, f32[64,512]{1,0:T(8,128)}, f32[64,512]{1,0:T(8,128)}, f32[48,64]{1,0:T(8,128)}) custom-call(f32[64,512]{1,0:T(8,128)S(1)} %get-tuple-element.12.refs_0_, f32[64,512]{1,0:T(8,128)S(1)} %get-tuple-element.13.refs_1_, f32[64,512]{1,0:T(8,128)S(1)} %get-tuple-element.14.refs_2_, f32[48,64]{1,0:T(8,128)S(1)} %get-tuple-element.15.refs_3_), custom_call_target="tpu_custom_call" | custom-call | tf_op jit(solution)/shard_map/flush/pallas_call | solution.py:417

commit v5 on v4

--- a/solution.py
+++ b/solution.py
@@ -98,13 +98,16 @@
     for copy in loads:
         copy.wait()
 
-    def row_copy(k):
-        source = (HALO, rows)[k]
-        target = (HALO + rows, 0)[k]
+    near = HALO // 2
+
+    def row_copy(k, part):
+        shift = near * (part if k == 0 else 1 - part)
+        source = (HALO, rows)[k] + shift
+        target = (HALO + rows, 0)[k] + shift
         return pltpu.make_async_remote_copy(
-            wide.at[:, :, source:source + HALO, :],
-            wide.at[:, :, target:target + HALO, :],
-            row_send.at[k], row_recv.at[k],
+            wide.at[:, :, source:source + near, :],
+            wide.at[:, :, target:target + near, :],
+            row_send.at[k, part], row_recv.at[k, part],
             device_id=(a + (-1, 1)[k], b), device_id_type=MESH)
 
     def corner_copy(v, k):
@@ -146,11 +149,13 @@
 
     @pl.when(has_up)
     def _():
-        row_copy(0).start()
+        row_copy(0, 0).start()
+        row_copy(0, 1).start()
 
     @pl.when(has_down)
     def _():
-        row_copy(1).start()
+        row_copy(1, 0).start()
+        row_copy(1, 1).start()
 
     @pl.when(has_right)
     def _():
@@ -250,9 +255,14 @@
         sweep(s, first + half_halo, last - half_halo)
         return carry
 
-    def rim_early(s, carry):
-        sweep(s, 0, first + half_halo, exact_ahead=True)
-        sweep(s, last - half_halo, last + first, exact_above=True)
+    def rim_inner(s, carry):
+        sweep(s, half_halo, first + half_halo, exact_ahead=True)
+        sweep(s, last - half_halo, last + half_halo, exact_above=True)
+        return carry
+
+    def rim_outer(s, carry):
+        sweep(s, 0, first, exact_ahead=True)
+        sweep(s, last, last + first, exact_above=True)
         return carry
 
     def rim_late(s, carry):
@@ -273,25 +283,31 @@
         chooser[o] = jnp.concatenate(
             [jnp.where(lower, 1.0, 0.0), jnp.where(upper, 1.0, 0.0)], 1).astype(jnp.bfloat16)
 
-    @pl.when(has_up)
-    def _():
-        row_copy(0).wait_send()
-        row_copy(1).wait_recv()
-
-    @pl.when(has_down)
-    def _():
-        row_copy(1).wait_send()
-        row_copy(0).wait_recv()
-
+    def wait_rows(part):
+        @pl.when(has_up)
+        def _():
+            row_copy(0, part).wait_send()
+            row_copy(1, part).wait_recv()
+
+        @pl.when(has_down)
+        def _():
+            row_copy(1, part).wait_send()
+            row_copy(0, part).wait_recv()
+
+    wait_rows(0)
     for v, k in diagonals:
         @pl.when(toward(v, k))
         def _():
             corner_copy(v, k).wait_send()
             corner_copy(1 - v, 1 - k).wait_recv()
 
-    prepare(0, HALO)
-    prepare(HALO + rows, tall)
-    lax.fori_loop(0, middle_step, rim_early, 0)
+    prepare(near, HALO)
+    prepare(HALO + rows, HALO + rows + near)
+    lax.fori_loop(0, middle_step, rim_inner, 0)
+    wait_rows(1)
+    prepare(0, near)
+    prepare(HALO + rows + near, tall)
+    lax.fori_loop(0, middle_step, rim_outer, 0)
     lax.fori_loop(middle_step, STEPS, rim_late, 0)
 
     slot_lane = lax.broadcasted_iota(jnp.int32, (STEPS, slots), 1)
@@ -407,7 +423,7 @@
                 pltpu.VMEM((n_gy, 2 * GAUGE_DEV, 2 * slots), jnp.bfloat16),
                 pltpu.VMEM((3 * STEPS, GAUGE_DEV), jnp.float32),
                 pltpu.VMEM((1, slots), jnp.int32), pltpu.SMEM((1, slots), jnp.int32),
-                dma((5, chunks)), dma((2,)), dma((2,)), dma((2,)), dma((2,)),
+                dma((5, chunks)), dma((2, 2)), dma((2, 2)), dma((2,)), dma((2,)),
                 dma((2, 2)), dma((2, 2)), dma((n_gy,)), dma((n_gy,)), dma((3, chunks + 1)), dma((2,)),
             ],
             compiler_params=pltpu.CompilerParams(collective_id=0, has_side_effects=True,

time: 25 us -> 24.9 us (level)
  no operation moved by 1% of the time
where the time goes in v5:
time: 24.9 us; the launch traced here: 24.7 us
  Pallas kernels  24.1 us (97%)
  between operations  0.64 us (3%)
    pallas_call x1, Pallas kernels, shards(): pl.pallas_call(lambda *refs: kernel(n_gx, n_gy, *refs), name='window', ou...  23.3 us
    pallas_call x1, Pallas kernels, shards(): pl.pallas_call(flush, name='flush', out_shape=(field, field, field, serie...  0.78 us

profile of v5, /device:TPU:5, one launch (start us, length us, event | category | flops | bytes accessed | tf_op | source)
XLA Modules:
  0.0 24.7 jit_solution(2227569792526386434)
XLA Ops:
  0.6 23.3 %window.1 = (f32[64,512]{1,0:T(8,128)S(1)}, f32[64,512]{1,0:T(8,128)S(1)}, f32[64,512]{1,0:T(8,128)S(1)}, f32[48,64]{1,0:T(8,128)S(1)}) custom-call(f32[64,512]{1,0:T(8,128)} %refs_0_.1, f32[64,512]{1,0:T(8,128)} %refs_1_.1, f32[64,512]{1,0:T(8,128)} %refs_2_.1, f32[64,512]{1,0:T(8,128)} %refs_3_.1, f32[64,512]{1,0:T(8,128)} %refs_4_.1, s32[1,128]{1,0:T(1,128)} %refs_5_.1, ...), custom_call_target="tpu_custom_call" | custom-call | tf_op jit(solution)/shard_map/window/pallas_call | solution.py:408
  23.9 0.8 %flush.1 = (f32[64,512]{1,0:T(8,128)}, f32[64,512]{1,0:T(8,128)}, f32[64,512]{1,0:T(8,128)}, f32[48,64]{1,0:T(8,128)}) custom-call(f32[64,512]{1,0:T(8,128)S(1)} %get-tuple-element.12.refs_0_, f32[64,512]{1,0:T(8,128)S(1)} %get-tuple-element.13.refs_1_, f32[64,512]{1,0:T(8,128)S(1)} %get-tuple-element.14.refs_2_, f32[48,64]{1,0:T(8,128)S(1)} %get-tuple-element.15.refs_3_), custom_call_target="tpu_custom_call" | custom-call | tf_op jit(solution)/shard_map/flush/pallas_call | solution.py:433
